TPU v7x, 32 devices: a whole 2x2x4 slice. The times are simulated.
32 devices in a mesh: grp: 2 (over y), req: 8 (over z, x), head: 2 (over core).
Axes of the slice: x: 2, y: 2, z: 4, core: 2. Of those that a mesh axis runs over, the one named last changes fastest.
Arguments:
- draft_input: bfloat16 [1024, 8192], P(('grp', 'req'), 'head'), parts along dimension 0, may hold values from -4.5 to 4.5
- draft_proj: bfloat16 [1024, 2048], P(('grp', 'req'), 'head'), parts along dimension 0, may hold values from -4.5 to 4.5
- draft_step: bfloat16 [1024, 128], P(('grp', 'req'), 'head'), parts along dimension 0, may hold values from -4 to 4
- draft_query: bfloat16 [1024, 4096], P(('grp', 'req'), 'head'), parts along dimension 0, may hold values from -120 to 120
- draft_keyval: bfloat16 [1024, 1024], P(('grp', 'req'), 'head'), parts along dimension 0, may hold values from -4.5 to 4.5
- row_target: int32 [1024], P(('grp', 'req')), parts along dimension 0, may hold values from 0 to 511, as said below
- tree_mask: int32 [16, 64, 64], P(('grp', 'req')), parts along dimension 0, may hold values from 0 to 1, as said below
- accepted: int32 [16], P(('grp', 'req')), parts along dimension 0, may hold values from 0 to 63
- cache_length: int32 [16], P(('grp', 'req')), parts along dimension 0, may hold values from 1 to 1024, as said below
- scan_state: bfloat16 [16, 128, 64, 128], P(('grp', 'req'), 'head'), parts along dimension 0, may hold values from -10.5 to 10.5
- cache_keyval: bfloat16 [16, 1024, 1024], P(('grp', 'req'), None, 'head'), parts along dimension 0, may hold values from -4.5 to 4.5
- decay_rate: float32 [128], P('head'), may hold values from 0.02 to 1.5
- step_bias: float32 [128], P('head'), may hold values from -3.5 to -1.5
- skip_gain: float32 [128], P('head'), may hold values from 0.5 to 1.5
- norm_gain: float32 [8192], P('head'), may hold values from 0.5 to 1.5
Outputs:
- mixer_out: bfloat16 [1024, 8192], P(('grp', 'req'), 'head'), parts along dimension 0
- attend_out: bfloat16 [1024, 4096], P(('grp', 'req'), 'head'), parts along dimension 0
- accepted_state: bfloat16 [16, 128, 64, 128], P(('grp', 'req'), 'head'), parts along dimension 0
There are 2 independent parts, one for each index of `grp`. A program takes and returns all parts, laid end to end along the dimension named above; an argument that names none is the same for every part. Nothing has to cross between parts.
Inputs may be any that keep to these rules, and one draw needn't show every extreme that they name: `row_target`: A permutation of all rows. The owner of row g is g // 64. Of the 64 rows of one drafter device at most 8 go to any one owner, and some drafter sends exactly 8 to some owner. tree_mask[r,i,j] is 1 exactly when node j is node i or an ancestor of node i; node 0 is the root and every parent has a smaller index than its child. `cache_length`: some request uses all 1024 positions.
All inputs are finite; a program needn't handle non-finite values.
Results may differ from a plain program's by a relative error of at most 0.0049.
Values may be sent and summed in bfloat16 or wider, within the bound.
No kernel may reach another device: no remote copies, remote signals or barrier semaphores. Data moves between devices by JAX's collectives and lax.ppermute only.
A program may use at most 128 MiB of HBM per device.

v0:
```python
import functools

import jax
import jax.numpy as jnp
from jax import lax
from jax.experimental import pallas as pl
from jax.experimental.pallas import tpu as pltpu
from jax.sharding import PartitionSpec as P


HEAD_DIM = 64
STATE = 128
QDIM = 128
NODES = 64
LANES = 128
F32 = jnp.float32
BF16 = jnp.bfloat16


def last_dot(left, right):
    return lax.dot_general(left, right, (((1,), (1,)), ((), ())), preferred_element_type=F32)


def row_to_column(row):
    size = row.shape[1]
    sub = lax.broadcasted_iota(jnp.int32, (size, size), 0)
    lane = lax.broadcasted_iota(jnp.int32, (size, size), 1)
    spread = jnp.broadcast_to(row, (size, size))
    return jnp.sum(jnp.where(sub == lane, spread, jnp.zeros_like(spread)), axis=1, keepdims=True)


def slot_one_hot(target, row_count, cap_rows, slot_total, me):
    shift = row_count.bit_length() - 1
    peer = lax.shift_right_logical(target, jnp.full_like(target, shift))
    local = target - peer * row_count
    peer_f = peer.astype(F32)
    peer_col = row_to_column(peer_f)
    size = row_count
    sub = lax.broadcasted_iota(jnp.int32, (size, size), 0)
    lane = lax.broadcasted_iota(jnp.int32, (size, size), 1)
    same = jnp.logical_and(peer_col == peer_f, sub < lane)
    rank = jnp.sum(jnp.where(same, 1.0, 0.0), axis=0, keepdims=True).astype(jnp.int32)
    block = peer if me is None else jnp.bitwise_xor(peer, jnp.full_like(peer, me))
    slot = block * cap_rows + rank
    slots = lax.broadcasted_iota(jnp.int32, (slot_total, size), 0)
    return jnp.where(slots == slot, 1.0, 0.0).astype(BF16), local


def pack(sizes, xor_blocks, layout, *refs):
    row_count, cap_rows, block_count = sizes
    target_hbm, sources, refs = refs[0], refs[1:6], refs[6:]
    outs, held_target, held, sems = refs[:-7], refs[-7], refs[-6:-1], refs[-1]
    target_copy = pltpu.make_async_copy(target_hbm, held_target, sems.at[5])
    target_copy.start()
    copies = [
        pltpu.make_async_copy(source, buffer, sems.at[index])
        for index, (source, buffer) in enumerate(zip(sources, held))
    ]
    for copy in copies:
        copy.start()
    me = lax.axis_index("req") if xor_blocks else None
    slot_total = block_count * cap_rows
    target_copy.wait()
    chosen, local = slot_one_hot(held_target[...], row_count, cap_rows, slot_total, me)
    column = 0
    for index, buffer in enumerate(held):
        copies[index].wait()
        part = buffer[...]
        width = part.shape[1]
        if index == len(held) - 1:
            local_col = row_to_column((local + 1).astype(F32))
            labels = jnp.broadcast_to(local_col, (row_count, LANES - width)).astype(BF16)
            part = jnp.concatenate([part, labels], axis=1)
            width = LANES
        moved = jnp.dot(chosen, part, preferred_element_type=F32).astype(BF16)
        for out_ref, (first_block, blocks, start) in zip(outs, layout):
            if start <= column < start + out_ref.shape[1]:
                rows = slice(first_block * cap_rows, (first_block + blocks) * cap_rows)
                out_ref[:, column - start : column - start + width] = moved[rows]
        column += width


def joined(views, start, width):
    parts = [ref[:, start - offset : start - offset + width] for ref, offset in views]
    return parts[0] if len(parts) == 1 else jnp.concatenate(parts, axis=0)


def middle(offsets, sizes, *refs):
    query_width, keyval_width, proj_width, head_local, query_start = sizes
    blocks, refs = tuple(zip(refs, offsets)), refs[len(offsets) :]
    scalar_ref, mask_hbm, decay_hbm, bias_hbm, skip_hbm, state_hbm, cache_hbm, gain_hbm = refs[:8]
    attend_hbm, weight_ref, base_ref, path_ref, kept_ref = refs[8:13]
    write_ref, order_ref, skip_out_ref, gain_ref = refs[13:17]
    mask_ref, decay_ref, bias_ref, skip_ref, state_ref, cache_ref = refs[17:23]
    attend_ref, score_ref, prob_ref, sems, out_sems = refs[23:]
    sources = (mask_hbm, decay_hbm, bias_hbm, skip_hbm, state_hbm, cache_hbm, gain_hbm)
    targets = (mask_ref, decay_ref, bias_ref, skip_ref, state_ref, cache_ref, gain_ref)
    loads = [
        pltpu.make_async_copy(source, held, sems.at[index])
        for index, (source, held) in enumerate(zip(sources, targets))
    ]
    for load in loads:
        load.start()
    nodes = mask_ref.shape[1]
    kv_start = query_start + query_width
    proj_start = kv_start + keyval_width
    step_start = proj_start + proj_width
    tail = joined(blocks, step_start, LANES)
    label_lane = tail[:, LANES - nodes :].astype(F32)
    slot_total = tail.shape[0]
    node_lane = lax.broadcasted_iota(jnp.int32, (slot_total, nodes), 1).astype(F32) + 1.0
    order = jnp.where(label_lane == node_lane, 1.0, 0.0).T.astype(BF16)
    order_ref[...] = order

    def ordered(start, width):
        return jnp.dot(order, joined(blocks, start, width), preferred_element_type=F32)

    for load in loads[:4]:
        load.wait()
    mask_float = mask_ref[0].astype(F32)
    raw = ordered(step_start, LANES)[:, :head_local] + bias_ref[...]
    step = jnp.maximum(raw, 0.0) + jnp.log1p(jnp.exp(-jnp.abs(raw)))
    cumulative = jnp.dot(
        mask_float,
        -decay_ref[...] * step,
        precision=lax.Precision.HIGHEST,
        preferred_element_type=F32,
    )
    cumulative_t = cumulative.T
    step_t = step.T
    accepted = scalar_ref[0:1, 0:1]
    node_sub = lax.broadcasted_iota(jnp.int32, (nodes, head_local), 0)
    lane_of = lax.broadcasted_iota(jnp.int32, (head_local, nodes), 1)
    pick = jnp.sum(jnp.where(node_sub == accepted, cumulative, 0.0), axis=0, keepdims=True)
    node_lanes = lax.broadcasted_iota(jnp.int32, (nodes, nodes), 1)
    mask_pick = jnp.sum(
        jnp.where(node_lanes == accepted, mask_float.T, 0.0), axis=1, keepdims=True
    )
    path = mask_pick * jnp.exp(jnp.minimum(pick - cumulative, 0.0)) * step
    pick_col = jnp.sum(jnp.where(lane_of == accepted, cumulative_t, 0.0), axis=1, keepdims=True)
    keep = jnp.broadcast_to(jnp.exp(pick_col), (head_local, LANES))
    skip_row = skip_ref[...]

    groups = proj_width // (2 * STATE)
    per_group = head_local // groups
    wide = LANES // HEAD_DIM
    low = lax.broadcasted_iota(jnp.int32, (nodes, LANES), 1) < HEAD_DIM
    low_row = lax.broadcasted_iota(jnp.int32, (1, LANES), 1) < HEAD_DIM

    def spread(table, head, rows_low):
        return jnp.where(rows_low, table[:, head : head + 1], table[:, head + 1 : head + 2])

    def pair_row(table, head):
        return jnp.concatenate([table[head : head + 1], table[head + 1 : head + 2]], axis=1)

    loads[4].wait()
    for group in range(groups):
        proj = ordered(proj_start + group * 2 * STATE, 2 * STATE).astype(BF16)
        write_rows = proj[:, :STATE]
        read_rows = proj[:, STATE:]
        write_ref[:, group * STATE : (group + 1) * STATE] = write_rows
        inner = last_dot(read_rows, write_rows) * mask_float
        inner = jnp.concatenate([inner] * wide, axis=1)
        state = state_ref[0, group * per_group : (group + 1) * per_group]
        carried = last_dot(read_rows, state.reshape(per_group * HEAD_DIM, STATE))
        for pair in range(per_group // wide):
            head = group * per_group + pair * wide
            lanes = slice(head * HEAD_DIM, head * HEAD_DIM + LANES)
            decay_i = spread(cumulative, head, low)
            decay_j = pair_row(cumulative_t, head)
            step_j = pair_row(step_t, head)
            weight = jnp.exp(jnp.minimum(decay_i - decay_j, 0.0)) * inner * step_j
            weight_ref[:, lanes] = weight.astype(BF16)
            base_ref[:, lanes] = (
                jnp.exp(decay_i) * carried[:, pair * LANES : (pair + 1) * LANES]
            )
            path_ref[:, lanes] = spread(path, head, low)
            skip_out_ref[:, lanes] = spread(skip_row, head, low_row)
    for head in range(head_local):
        kept_ref[head] = keep[head : head + 1, :] * state_ref[0, head].astype(F32)

    pair_heads = keyval_width // (2 * QDIM)
    group_size = query_width // QDIM // pair_heads
    cache_count = cache_ref.shape[1]
    query_scale = QDIM ** (-0.5)
    length = scalar_ref[1:2, 0:1]
    valid = lax.broadcasted_iota(jnp.int32, (1, cache_count), 1) < length
    tree_valid = mask_float > 0.0
    tree_pairs = ordered(kv_start, keyval_width).astype(BF16)
    loads[5].wait()
    stores = []
    for pair in range(pair_heads):
        first = pair * group_size * QDIM
        query = ordered(query_start + first, group_size * QDIM).astype(BF16)
        query = jnp.concatenate(
            [query[:, g * QDIM : (g + 1) * QDIM] for g in range(group_size)], axis=0
        )
        kcol = pair * 2 * QDIM
        keys = cache_ref[0, :, kcol : kcol + QDIM]
        values = cache_ref[0, :, kcol + QDIM : kcol + 2 * QDIM]
        score_ref[...] = last_dot(query, keys)
        tree_score = last_dot(query, tree_pairs[:, kcol : kcol + QDIM])
        sums = []
        tree_probs = []
        for g in range(group_size):
            rows = slice(g * nodes, (g + 1) * nodes)
            cache_part = jnp.where(valid, score_ref[rows, :], -1e30)
            tree_part = jnp.where(tree_valid, tree_score[rows], -1e30)
            peak = jnp.maximum(
                jnp.max(cache_part, axis=1, keepdims=True),
                jnp.max(tree_part, axis=1, keepdims=True),
            )
            cache_exp = jnp.exp((cache_part - peak) * query_scale)
            tree_exp = jnp.exp((tree_part - peak) * query_scale)
            sums.append(
                jnp.sum(cache_exp, axis=1, keepdims=True)
                + jnp.sum(tree_exp, axis=1, keepdims=True)
            )
            prob_ref[rows, :] = cache_exp.astype(BF16)
            tree_probs.append(tree_exp.astype(BF16))
        result = jnp.dot(prob_ref[...], values, preferred_element_type=F32)
        result = result + jnp.dot(
            jnp.concatenate(tree_probs, axis=0),
            tree_pairs[:, kcol + QDIM : kcol + 2 * QDIM],
            preferred_element_type=F32,
        )
        for g in range(group_size):
            attend_ref[:, first + g * QDIM : first + (g + 1) * QDIM] = (
                result[g * nodes : (g + 1) * nodes] / sums[g]
            ).astype(BF16)
        lanes = pl.ds(first, group_size * QDIM)
        stores.append(
            pltpu.make_async_copy(
                attend_ref.at[:, lanes], attend_hbm.at[:, lanes], out_sems.at[pair]
            )
        )
        stores[-1].start()
    loads[6].wait()
    for store in stores:
        store.wait()


def mix(offsets, *refs):
    blocks, refs = tuple(zip(refs, offsets)), refs[len(offsets) :]
    order_ref, weight_ref, base_ref, path_ref, skip_ref = refs[:5]
    mixed_ref, square_ref, weighted_ref = refs[5:]
    nodes, width = mixed_ref.shape
    order = order_ref[...]
    sub = lax.broadcasted_iota(jnp.int32, (2 * nodes, LANES), 0) < nodes
    lane = lax.broadcasted_iota(jnp.int32, (2 * nodes, LANES), 1) < HEAD_DIM
    same = sub == lane
    total = jnp.zeros((nodes, LANES), F32)
    chunk = 4 * LANES
    for start in range(0, width, chunk):
        wide = jnp.dot(order, joined(blocks, start, chunk), preferred_element_type=F32)
        rows = wide.astype(BF16)
        for begin in range(0, chunk, LANES):
            lanes = slice(start + begin, start + begin + LANES)
            one = rows[:, begin : begin + LANES]
            one_wide = wide[:, begin : begin + LANES]
            both = jnp.concatenate([one, one], axis=0)
            both = jnp.where(same, both, jnp.zeros_like(both))
            mixed = jnp.dot(weight_ref[:, lanes], both, preferred_element_type=F32)
            mixed = mixed + base_ref[:, lanes] + skip_ref[:, lanes] * one_wide
            mixed_ref[:, lanes] = mixed
            total = total + mixed * mixed
            weighted_ref[:, lanes] = (path_ref[:, lanes] * one_wide).astype(BF16)
    square_ref[...] = jnp.broadcast_to(jnp.sum(total, axis=1, keepdims=True), square_ref.shape)


def advance(weighted_ref, write_ref, kept_ref, out_hbm, out_ref, sems):
    head_local = kept_ref.shape[0]
    groups = write_ref.shape[1] // STATE
    per_group = head_local // groups
    width = per_group * HEAD_DIM
    stores = []
    for group in range(groups):
        update = lax.dot_general(
            weighted_ref[:, group * width : (group + 1) * width],
            write_ref[:, group * STATE : (group + 1) * STATE],
            (((0,), (0,)), ((), ())),
            preferred_element_type=F32,
        )
        for index in range(per_group):
            head = group * per_group + index
            out_ref[0, head] = (
                kept_ref[head] + update[index * HEAD_DIM : (index + 1) * HEAD_DIM]
            ).astype(BF16)
        heads = pl.ds(group * per_group, per_group)
        stores.append(
            pltpu.make_async_copy(out_ref.at[:, heads], out_hbm.at[:, heads], sems.at[group])
        )
        stores[-1].start()
    for store in stores:
        store.wait()


def normalise(total_width, mixed_ref, mine_ref, other_ref, gain_ref, out_hbm, out_ref, sems):
    square = mine_ref[...] + other_ref[...]
    scale = 1.0 / jnp.sqrt(square / total_width + 1e-05)
    chunks = sems.shape[0]
    width = out_ref.shape[1] // chunks
    stores = []
    for chunk in range(chunks):
        for start in range(chunk * width, (chunk + 1) * width, LANES):
            lanes = slice(start, start + LANES)
            out_ref[:, lanes] = (mixed_ref[:, lanes] * scale * gain_ref[:, lanes]).astype(BF16)
        view = pl.ds(chunk * width, width)
        stores.append(
            pltpu.make_async_copy(out_ref.at[:, view], out_hbm.at[:, view], sems.at[chunk])
        )
        stores[-1].start()
    for store in stores:
        store.wait()


SPACES = {"h": pltpu.HBM, "v": pltpu.VMEM, "s": pltpu.SMEM}


def call(body, ins, outs, scratch=(), mebibytes=8):
    def run(*operands):
        placed = [
            operand if space == "s" else pltpu.with_memory_space_constraint(operand, SPACES[space])
            for space, operand in zip(ins, operands, strict=True)
        ]
        return pl.pallas_call(
            body,
            out_shape=tuple(SPACES[space](dims, kind) for space, dims, kind in outs),
            in_specs=[pl.BlockSpec(memory_space=SPACES[space]) for space in ins],
            out_specs=tuple(pl.BlockSpec(memory_space=SPACES[out[0]]) for out in outs),
            scratch_shapes=scratch,
            compiler_params=pltpu.CompilerParams(vmem_limit_bytes=mebibytes * 1024 * 1024),
        )(*placed)

    return run


def local(
    draft_input,
    draft_proj,
    draft_step,
    draft_query,
    draft_keyval,
    row_target,
    tree_mask,
    accepted,
    cache_length,
    scan_state,
    cache_keyval,
    decay_rate,
    step_bias,
    skip_gain,
    norm_gain,
):
    row_count, scan_width = draft_input.shape
    peers = lax.axis_size("req")
    head_shards = lax.axis_size("head")
    cap_rows = max(2, row_count // peers)
    slot_total = peers * cap_rows
    direct = peers <= 16 and peers & (peers - 1) == 0
    head_local = scan_width // HEAD_DIM
    query_width = draft_query.shape[1]
    keyval_width = draft_keyval.shape[1]
    proj_width = draft_proj.shape[1]
    groups = proj_width // (2 * STATE)
    all_width = scan_width + query_width + keyval_width + proj_width + LANES
    near = peers // 2 if direct else 0
    if direct:
        layout = [(block, 1, 0) for block in range(near)]
        layout += [(block, 1, scan_width) for block in range(near, peers)]
        layout += [(block, 1, 0) for block in range(near, peers)]
        widths = [all_width] * near + [all_width - scan_width] * (peers - near)
        widths += [scan_width] * (peers - near)
    else:
        layout, widths = [(0, peers, 0)], [all_width]
    sources = (draft_input, draft_query, draft_keyval, draft_proj, draft_step)
    packed = call(
        functools.partial(pack, (row_count, cap_rows, peers), direct, layout),
        "h" * 6,
        tuple(
            ("v", (blocks * cap_rows, width), BF16)
            for (_, blocks, _), width in zip(layout, widths)
        ),
        scratch=[pltpu.VMEM((1, row_count), jnp.int32)]
        + [pltpu.VMEM(source.shape, BF16) for source in sources]
        + [pltpu.SemaphoreType.DMA((6,))],
    )(row_target.reshape(1, row_count), *sources)

    def moved(block, step):
        pairs = [(index, index ^ step) for index in range(peers)]
        return lax.ppermute(block, "req", pairs)

    if direct:
        whole = [packed[0]] + [moved(packed[step], step) for step in range(1, near)]
        far = range(near, peers)
        firsts = [moved(packed[step], step) for step in far]
        seconds = [moved(packed[step + peers - near], step) for step in far]
        first_blocks, first_offsets = whole + firsts, [0] * near + [scan_width] * len(far)
        second_blocks, second_offsets = whole + seconds, [0] * peers
    else:
        split = packed[0].reshape(peers, cap_rows, all_width)
        arrived = lax.all_to_all(split, "req", split_axis=0, concat_axis=0, tiled=True)
        first_blocks = second_blocks = [arrived.reshape(slot_total, all_width)]
        first_offsets = second_offsets = [0]

    scalars = jnp.broadcast_to(jnp.stack([accepted, cache_length]), (2, LANES))
    pair_heads = keyval_width // (2 * QDIM)
    score_rows = NODES * (query_width // QDIM // pair_heads)
    cache_count = cache_keyval.shape[1]
    attend_out, weight, base, path, kept, write, order, skip_wide, gain = call(
        functools.partial(
            middle,
            first_offsets,
            (query_width, keyval_width, proj_width, head_local, scan_width),
        ),
        "v" * (len(first_blocks) + 1) + "h" * 7,
        (
            ("h", (row_count, query_width), BF16),
            ("v", (NODES, head_local * NODES), BF16),
            ("v", (NODES, scan_width), F32),
            ("v", (NODES, scan_width), F32),
            ("v", (head_local, HEAD_DIM, STATE), F32),
            ("v", (NODES, groups * STATE), BF16),
            ("v", (NODES, slot_total), BF16),
            ("v", (1, scan_width), F32),
            ("v", (1, scan_width), F32),
        ),
        scratch=[
            pltpu.VMEM(tree_mask.shape, jnp.int32),
            pltpu.VMEM((1, head_local), F32),
            pltpu.VMEM((1, head_local), F32),
            pltpu.VMEM((1, head_local), F32),
            pltpu.VMEM(scan_state.shape, BF16),
            pltpu.VMEM(cache_keyval.shape, BF16),
            pltpu.VMEM((row_count, query_width), BF16),
            pltpu.VMEM((score_rows, cache_count), F32),
            pltpu.VMEM((score_rows, cache_count), BF16),
            pltpu.SemaphoreType.DMA((7,)),
            pltpu.SemaphoreType.DMA((pair_heads,)),
        ],
        mebibytes=24,
    )(
        *first_blocks,
        scalars,
        tree_mask,
        decay_rate.reshape(1, head_local),
        step_bias.reshape(1, head_local),
        skip_gain.reshape(1, head_local),
        scan_state,
        cache_keyval,
        norm_gain.reshape(1, scan_width),
    )

    mixed, square, weighted = call(
        functools.partial(mix, second_offsets),
        "v" * (len(second_blocks) + 5),
        (
            ("v", (NODES, scan_width), F32),
            ("v", (NODES, LANES), F32),
            ("v", (NODES, scan_width), BF16),
        ),
    )(*second_blocks, order, weight, base, path, skip_wide)
    swap = [(index, (index + 1) % head_shards) for index in range(head_shards)]
    other = lax.ppermute(square, "head", swap)
    new_state = call(
        advance,
        "v" * 3,
        (("h", scan_state.shape, BF16),),
        scratch=[pltpu.VMEM(scan_state.shape, BF16), pltpu.SemaphoreType.DMA((groups,))],
    )(weighted, write, kept)[0]
    mixer_out = call(
        functools.partial(normalise, head_shards * scan_width),
        "v" * 4,
        (("h", (row_count, scan_width), BF16),),
        scratch=[pltpu.VMEM((row_count, scan_width), BF16), pltpu.SemaphoreType.DMA((groups,))],
    )(mixed, square, other, gain)[0]
    return (mixer_out, attend_out, new_state)


def solution(mesh):
    assert mesh.shape["head"] == 2
    rows = P(("grp", "req"), "head")

    return jax.shard_map(
        local,
        mesh=mesh,
        in_specs=(
            rows,
            rows,
            rows,
            rows,
            rows,
            P(("grp", "req")),
            P(("grp", "req"), None, None),
            P(("grp", "req")),
            P(("grp", "req")),
            P(("grp", "req"), "head", None, None),
            P(("grp", "req"), None, "head"),
            P("head"),
            P("head"),
            P("head"),
            P("head"),
        ),
        out_specs=(rows, rows, P(("grp", "req"), "head", None, None)),
        check_vma=False,
    )
```

profile of v0, /device:TPU:0, one launch (start us, length us, event | category | flops | bytes accessed | tf_op | source)
XLA Modules:
  0.0 38.9 jit_solution(10441593918764274318)
XLA Ops:
  0.6 2.1 %shard_map.166 = (bf16[8,7808]{1,0:T(8,128)(2,1)S(1)}, bf16[8,7808]{1,0:T(8,128)(2,1)S(1)}, bf16[8,7808]{1,0:T(8,128)(2,1)S(1)}, bf16[8,7808]{1,0:T(8,128)(2,1)S...) custom-call(s32[1,64]{1,0:T(1,128)} %bitcast.12, ...), custom_call_target="tpu_custom_call" | custom-call | tf_op jit(solution)/shard_map/pallas_call | solution.py:326
  2.8 3.0 %collective-permute-start = (bf16[8,7808]{1,0:T(8,128)(2,1)S(1)}, bf16[8,7808]{1,0:T(8,128)(2,1)S(1)}, u32[]{:S(2)}, u32[]{:S(2)}) collective-permute-start(bf16[8,7808]{1,0:T(8,128)(2,1)S(1)} %get-tuple-element.28), channel_id=1, source_target_pairs={{0,2},{2,0},{4,6},{6,4},{8,10},{10,8},{12,14},{14,12},{1,3},{3,1},... | collective-permute-start | bytes 374792 | tf_op jit(solution)/shard_map/ppermute | solution.py:391
  5.8 1.6 %collective-permute-start.1 = (bf16[8,7808]{1,0:T(8,128)(2,1)S(1)}, bf16[8,7808]{1,0:T(8,128)(2,1)S(1)}, u32[]{:S(2)}, u32[]{:S(2)}) collective-permute-start(bf16[8,7808]{1,0:T(8,128)(2,1)S(1)} %get-tuple-element.29), channel_id=1, source_target_pairs={{0,4},{2,6},{4,0},{6,2},{8,12},{10,14},{12,8},{14,10},{1,5},{3,7},... | collective-permute-start | bytes 374792 | tf_op jit(solution)/shard_map/ppermute | solution.py:391
  7.4 2.6 %collective-permute-start.7 = (bf16[8,3712]{1,0:T(8,128)(2,1)S(1)}, bf16[8,3712]{1,0:T(8,128)(2,1)S(1)}, u32[]{:S(2)}, u32[]{:S(2)}) collective-permute-start(bf16[8,3712]{1,0:T(8,128)(2,1)S(1)} %get-tuple-element.35), channel_id=1, source_target_pairs={{0,8},{2,10},{4,12},{6,14},{8,0},{10,2},{12,4},{14,6},{1,9},{3,11}... | collective-permute-start | bytes 178184 | tf_op jit(solution)/shard_map/ppermute | solution.py:391
  10.0 0.3 collective-permute-start.8
  10.3 2.5 %collective-permute-start.9 = (bf16[8,3712]{1,0:T(8,128)(2,1)S(1)}, bf16[8,3712]{1,0:T(8,128)(2,1)S(1)}, u32[]{:S(2)}, u32[]{:S(2)}) collective-permute-start(bf16[8,3712]{1,0:T(8,128)(2,1)S(1)} %get-tuple-element.37), channel_id=1, source_target_pairs={{0,12},{2,14},{4,8},{6,10},{8,4},{10,6},{12,0},{14,2},{1,13},{3,15... | collective-permute-start | bytes 178184 | tf_op jit(solution)/shard_map/ppermute | solution.py:391
  12.7 1.1 %collective-permute-done.7.refs_4_ = bf16[8,3712]{1,0:T(8,128)(2,1)S(1)} collective-permute-done((bf16[8,3712]{1,0:T(8,128)(2,1)S(1)}, bf16[8,3712]{1,0:T(8,128)(2,1)S(1)}, u32[]{:S(2)}, u32[]{:S(2)}) %collective-permute-start.7) | collective-permute-done | bytes 59424 | tf_op jit(solution)/shard_map/ppermute | solution.py:391
  13.8 4.6 %collective-permute-start.10 = (bf16[8,3712]{1,0:T(8,128)(2,1)S(1)}, bf16[8,3712]{1,0:T(8,128)(2,1)S(1)}, u32[]{:S(2)}, u32[]{:S(2)}) collective-permute-start(bf16[8,3712]{1,0:T(8,128)(2,1)S(1)} %get-tuple-element.38), channel_id=1, source_target_pairs={{0,14},{2,12},{4,10},{6,8},{8,6},{10,4},{12,2},{14,0},{1,15},{3,13... | collective-permute-start | bytes 178184 | tf_op jit(solution)/shard_map/ppermute | solution.py:391
  18.4 0.0 collective-permute-done.8.refs_5_
  18.4 0.0 collective-permute-start.2
  19.7 0.0 collective-permute-done.9.refs_6_
  19.8 3.8 %collective-permute-start.3 = (bf16[8,4096]{1,0:T(8,128)(2,1)S(1)}, bf16[8,4096]{1,0:T(8,128)(2,1)S(1)}, u32[]{:S(2)}, u32[]{:S(2)}) collective-permute-start(bf16[8,4096]{1,0:T(8,128)(2,1)S(1)} %get-tuple-element.31), channel_id=1, source_target_pairs={{0,8},{2,10},{4,12},{6,14},{8,0},{10,2},{12,4},{14,6},{1,9},{3,11}... | collective-permute-start | bytes 196616 | tf_op jit(solution)/shard_map/ppermute | solution.py:391
  23.6 0.0 collective-permute-done.10.refs_7_
  23.6 1.1 %collective-permute-start.4 = (bf16[8,4096]{1,0:T(8,128)(2,1)S(1)}, bf16[8,4096]{1,0:T(8,128)(2,1)S(1)}, u32[]{:S(2)}, u32[]{:S(2)}) collective-permute-start(bf16[8,4096]{1,0:T(8,128)(2,1)S(1)} %get-tuple-element.32), channel_id=1, source_target_pairs={{0,10},{2,8},{4,14},{6,12},{8,2},{10,0},{12,6},{14,4},{1,11},{3,9}... | collective-permute-start | bytes 196616 | tf_op jit(solution)/shard_map/ppermute | solution.py:391
  24.7 0.0 collective-permute-done.refs_1_
  24.7 1.9 %collective-permute-start.5 = (bf16[8,4096]{1,0:T(8,128)(2,1)S(1)}, bf16[8,4096]{1,0:T(8,128)(2,1)S(1)}, u32[]{:S(2)}, u32[]{:S(2)}) collective-permute-start(bf16[8,4096]{1,0:T(8,128)(2,1)S(1)} %get-tuple-element.33), channel_id=1, source_target_pairs={{0,12},{2,14},{4,8},{6,10},{8,4},{10,6},{12,0},{14,2},{1,13},{3,15... | collective-permute-start | bytes 196616 | tf_op jit(solution)/shard_map/ppermute | solution.py:391
  26.6 0.0 collective-permute-done.1.refs_2_
  26.6 1.8 %collective-permute-start.6 = (bf16[8,4096]{1,0:T(8,128)(2,1)S(1)}, bf16[8,4096]{1,0:T(8,128)(2,1)S(1)}, u32[]{:S(2)}, u32[]{:S(2)}) collective-permute-start(bf16[8,4096]{1,0:T(8,128)(2,1)S(1)} %get-tuple-element.34), channel_id=1, source_target_pairs={{0,14},{2,12},{4,10},{6,8},{8,6},{10,4},{12,2},{14,0},{1,15},{3,13... | collective-permute-start | bytes 196616 | tf_op jit(solution)/shard_map/ppermute | solution.py:391
  28.4 0.1 add_bitcast_fusion
  28.5 0.0 collective-permute-done.2.refs_3_
  28.5 0.1 broadcast_in_dim.8.refs_8_
  28.6 6.4 %shard_map.167 = (bf16[64,2048]{1,0:T(8,128)(2,1)}, bf16[64,4096]{1,0:T(8,128)(2,1)S(1)}, f32[64,4096]{1,0:T(8,128)S(1)}, f32[64,4096]{1,0:T(8,128)S(1)}, f32[64...) custom-call(bf16[8,7808]{1,0:T(8,128)(2,1)S(1)} %get-tuple-element.2, ...), custom_call_target="tpu_custom_call" | custom-call | tf_op jit(solution)/shard_map/pallas_call | solution.py:326
  34.9 0.0 collective-permute-done.3.refs_4_
  35.0 0.0 collective-permute-done.4.refs_5_
  35.0 0.0 collective-permute-done.5.refs_6_
  35.0 0.0 collective-permute-done.6.refs_7_
  35.0 1.7 %shard_map.168 = (f32[64,4096]{1,0:T(8,128)S(1)}, f32[64,128]{1,0:T(8,128)S(1)}, bf16[64,4096]{1,0:T(8,128)(2,1)S(1)}) custom-call(bf16[8,7808]{1,0:T(8,128)(2,1)S(1)} %get-tuple-element.27.refs_0_, bf16[8,7808]{1,0:T(8,128)(2,1)S(1)} %collective-permute-done.refs_1_, bf16[8,7808]{1,0:T(8,128)(2,1)S(1)} %collective-permute-done.1.refs_2_, ...), custom_call_target="tpu_custom_call" | custom-call | tf_op jit(solution)/shard_map/pallas_call | solution.py:326
  36.7 0.0 collective-permute-start.11
  36.7 1.3 %shard_map.170 = bf16[1,64,64,128]{3,2,1,0:T(8,128)(2,1)} custom-call(bf16[64,4096]{1,0:T(8,128)(2,1)S(1)} %get-tuple-element.48.weighted_ref, bf16[64,512]{1,0:T(8,128)(2,1)S(1)} %get-tuple-element.49.write_ref, f32[64,64,128]{2,1,0:T(8,128)S(1)} %get-tuple-element.50.kept_ref), custom_call_target="tpu_custom_call" | custom-call | tf_op jit(solution)/shard_map/pallas_call | solution.py:326
  38.0 0.0 collective-permute-done.11.other_ref
  38.1 0.9 %shard_map.169 = bf16[64,4096]{1,0:T(8,128)(2,1)} custom-call(f32[64,4096]{1,0:T(8,128)S(1)} %get-tuple-element.44.mixed_ref, f32[64,128]{1,0:T(8,128)S(1)} %get-tuple-element.45.mine_ref, f32[64,128]{1,0:T(8,128)S(1)} %collective-permute-done.11.other_ref, f32[1,4096]{1,0:T(1,128)S(1)} %get-tuple-element.46.gain_ref), custom_call_target="tpu_custom_call" | custom-call | tf_op jit(solution)/shard_map/pallas_call | solution.py:326
Async XLA Ops:
  2.8 21.9 %collective-permute-start = (bf16[8,7808]{1,0:T(8,128)(2,1)S(1)}, bf16[8,7808]{1,0:T(8,128)(2,1)S(1)}, u32[]{:S(2)}, u32[]{:S(2)}) collective-permute-start(bf16[8,7808]{1,0:T(8,128)(2,1)S(1)} %get-tuple-element.28), channel_id=1, source_target_pairs={{0,2},{2,0},{4,6},{6,4},{8,10},{10,8},{12,14},{14,12},{1,3},{3,1},... | collective-permute-start | bytes 374792 | tf_op jit(solution)/shard_map/ppermute | solution.py:391
  5.8 20.8 %collective-permute-start.1 = (bf16[8,7808]{1,0:T(8,128)(2,1)S(1)}, bf16[8,7808]{1,0:T(8,128)(2,1)S(1)}, u32[]{:S(2)}, u32[]{:S(2)}) collective-permute-start(bf16[8,7808]{1,0:T(8,128)(2,1)S(1)} %get-tuple-element.29), channel_id=1, source_target_pairs={{0,4},{2,6},{4,0},{6,2},{8,12},{10,14},{12,8},{14,10},{1,5},{3,7},... | collective-permute-start | bytes 374792 | tf_op jit(solution)/shard_map/ppermute | solution.py:391
  7.4 6.4 %collective-permute-start.7 = (bf16[8,3712]{1,0:T(8,128)(2,1)S(1)}, bf16[8,3712]{1,0:T(8,128)(2,1)S(1)}, u32[]{:S(2)}, u32[]{:S(2)}) collective-permute-start(bf16[8,3712]{1,0:T(8,128)(2,1)S(1)} %get-tuple-element.35), channel_id=1, source_target_pairs={{0,8},{2,10},{4,12},{6,14},{8,0},{10,2},{12,4},{14,6},{1,9},{3,11}... | collective-permute-start | bytes 178184 | tf_op jit(solution)/shard_map/ppermute | solution.py:391
  10.0 8.5 %collective-permute-start.8 = (bf16[8,3712]{1,0:T(8,128)(2,1)S(1)}, bf16[8,3712]{1,0:T(8,128)(2,1)S(1)}, u32[]{:S(2)}, u32[]{:S(2)}) collective-permute-start(bf16[8,3712]{1,0:T(8,128)(2,1)S(1)} %get-tuple-element.36), channel_id=1, source_target_pairs={{0,10},{2,8},{4,14},{6,12},{8,2},{10,0},{12,6},{14,4},{1,11},{3,9}... | collective-permute-start | bytes 178184 | tf_op jit(solution)/shard_map/ppermute | solution.py:391
  10.3 9.5 %collective-permute-start.9 = (bf16[8,3712]{1,0:T(8,128)(2,1)S(1)}, bf16[8,3712]{1,0:T(8,128)(2,1)S(1)}, u32[]{:S(2)}, u32[]{:S(2)}) collective-permute-start(bf16[8,3712]{1,0:T(8,128)(2,1)S(1)} %get-tuple-element.37), channel_id=1, source_target_pairs={{0,12},{2,14},{4,8},{6,10},{8,4},{10,6},{12,0},{14,2},{1,13},{3,15... | collective-permute-start | bytes 178184 | tf_op jit(solution)/shard_map/ppermute | solution.py:391
  13.8 9.8 %collective-permute-start.10 = (bf16[8,3712]{1,0:T(8,128)(2,1)S(1)}, bf16[8,3712]{1,0:T(8,128)(2,1)S(1)}, u32[]{:S(2)}, u32[]{:S(2)}) collective-permute-start(bf16[8,3712]{1,0:T(8,128)(2,1)S(1)} %get-tuple-element.38), channel_id=1, source_target_pairs={{0,14},{2,12},{4,10},{6,8},{8,6},{10,4},{12,2},{14,0},{1,15},{3,13... | collective-permute-start | bytes 178184 | tf_op jit(solution)/shard_map/ppermute | solution.py:391
  18.4 10.0 %collective-permute-start.2 = (bf16[8,7808]{1,0:T(8,128)(2,1)S(1)}, bf16[8,7808]{1,0:T(8,128)(2,1)S(1)}, u32[]{:S(2)}, u32[]{:S(2)}) collective-permute-start(bf16[8,7808]{1,0:T(8,128)(2,1)S(1)} %get-tuple-element.30), channel_id=1, source_target_pairs={{0,6},{2,4},{4,2},{6,0},{8,14},{10,12},{12,10},{14,8},{1,7},{3,5},... | collective-permute-start | bytes 374792 | tf_op jit(solution)/shard_map/ppermute | solution.py:391
  19.8 15.2 %collective-permute-start.3 = (bf16[8,4096]{1,0:T(8,128)(2,1)S(1)}, bf16[8,4096]{1,0:T(8,128)(2,1)S(1)}, u32[]{:S(2)}, u32[]{:S(2)}) collective-permute-start(bf16[8,4096]{1,0:T(8,128)(2,1)S(1)} %get-tuple-element.31), channel_id=1, source_target_pairs={{0,8},{2,10},{4,12},{6,14},{8,0},{10,2},{12,4},{14,6},{1,9},{3,11}... | collective-permute-start | bytes 196616 | tf_op jit(solution)/shard_map/ppermute | solution.py:391
  23.6 11.4 %collective-permute-start.4 = (bf16[8,4096]{1,0:T(8,128)(2,1)S(1)}, bf16[8,4096]{1,0:T(8,128)(2,1)S(1)}, u32[]{:S(2)}, u32[]{:S(2)}) collective-permute-start(bf16[8,4096]{1,0:T(8,128)(2,1)S(1)} %get-tuple-element.32), channel_id=1, source_target_pairs={{0,10},{2,8},{4,14},{6,12},{8,2},{10,0},{12,6},{14,4},{1,11},{3,9}... | collective-permute-start | bytes 196616 | tf_op jit(solution)/shard_map/ppermute | solution.py:391
  24.7 10.3 %collective-permute-start.5 = (bf16[8,4096]{1,0:T(8,128)(2,1)S(1)}, bf16[8,4096]{1,0:T(8,128)(2,1)S(1)}, u32[]{:S(2)}, u32[]{:S(2)}) collective-permute-start(bf16[8,4096]{1,0:T(8,128)(2,1)S(1)} %get-tuple-element.33), channel_id=1, source_target_pairs={{0,12},{2,14},{4,8},{6,10},{8,4},{10,6},{12,0},{14,2},{1,13},{3,15... | collective-permute-start | bytes 196616 | tf_op jit(solution)/shard_map/ppermute | solution.py:391
  26.6 8.4 %collective-permute-start.6 = (bf16[8,4096]{1,0:T(8,128)(2,1)S(1)}, bf16[8,4096]{1,0:T(8,128)(2,1)S(1)}, u32[]{:S(2)}, u32[]{:S(2)}) collective-permute-start(bf16[8,4096]{1,0:T(8,128)(2,1)S(1)} %get-tuple-element.34), channel_id=1, source_target_pairs={{0,14},{2,12},{4,10},{6,8},{8,6},{10,4},{12,2},{14,0},{1,15},{3,13... | collective-permute-start | bytes 196616 | tf_op jit(solution)/shard_map/ppermute | solution.py:391
  36.7 1.4 %collective-permute-start.11 = (f32[64,128]{1,0:T(8,128)S(1)}, f32[64,128]{1,0:T(8,128)S(1)}, u32[]{:S(2)}, u32[]{:S(2)}) collective-permute-start(f32[64,128]{1,0:T(8,128)S(1)} %get-tuple-element.45.mine_ref), channel_id=1, source_target_pairs={{0,1},{1,0},{2,3},{3,2},{4,5},{5,4},{6,7},{7,6},{8,9},{9,8},{10,11... | collective-permute-start | bytes 98312 | tf_op jit(solution)/shard_map/ppermute | solution.py:464
where the time goes:
time: 39.1 us; the launch traced here: 38.9 us
  starting transfers between devices  23.2 us (59%)
  Pallas kernels  12.4 us (32%)
  between operations  2.02 us (5%)
  waiting for transfers between devices  1.13 us (3%)
    ppermute x11, starting transfers between devices, moved(): return lax.ppermute(block, 'req', pairs)  23.2 us
    pallas_call x5, Pallas kernels, run(): pl.pallas_call(body, out_shape=tuple((SPACES[space](dims, kind) for space...  12.4 us
    ppermute x11, waiting for transfers between devices, moved(): return lax.ppermute(block, 'req', pairs)  1.12 us
  transfers between devices with their start and end apart: 12, of which 1 were waited for; matrix products, arithmetic and copies ran while one was open for 0% of the time, Pallas kernels for 20%

commit v1 on v0

v1 whole, which is shorter than its diff:
```python
import functools

import jax
import jax.numpy as jnp
from jax import lax
from jax.experimental import pallas as pl
from jax.experimental.pallas import tpu as pltpu
from jax.sharding import PartitionSpec as P


HEAD_DIM = 64
STATE = 128
QDIM = 128
NODES = 64
LANES = 128
LOG2E = 1.4426950408889634
FAR = -1e30
EARLY = 0.0
F32 = jnp.float32
BF16 = jnp.bfloat16


def last_dot(left, right):
    return lax.dot_general(left, right, (((1,), (1,)), ((), ())), preferred_element_type=F32)


def row_to_column(row):
    size = row.shape[1]
    sub = lax.broadcasted_iota(jnp.int32, (size, size), 0)
    lane = lax.broadcasted_iota(jnp.int32, (size, size), 1)
    spread = jnp.broadcast_to(row, (size, size))
    return jnp.sum(jnp.where(sub == lane, spread, jnp.zeros_like(spread)), axis=1, keepdims=True)


def slot_one_hot(target, row_count, cap_rows, slot_total, me):
    shift = row_count.bit_length() - 1
    peer = lax.shift_right_logical(target, jnp.full_like(target, shift))
    local = target - peer * row_count
    peer_f = peer.astype(F32)
    peer_col = row_to_column(peer_f)
    size = row_count
    sub = lax.broadcasted_iota(jnp.int32, (size, size), 0)
    lane = lax.broadcasted_iota(jnp.int32, (size, size), 1)
    same = jnp.logical_and(peer_col == peer_f, sub < lane)
    rank = jnp.sum(jnp.where(same, 1.0, 0.0), axis=0, keepdims=True).astype(jnp.int32)
    block = peer if me is None else jnp.bitwise_xor(peer, jnp.full_like(peer, me))
    slot = block * cap_rows + rank
    slots = lax.broadcasted_iota(jnp.int32, (slot_total, size), 0)
    return jnp.where(slots == slot, 1.0, 0.0).astype(BF16), local


def pack(sizes, xor_blocks, layout, *refs):
    row_count, cap_rows, block_count = sizes
    target_hbm, sources, refs = refs[0], refs[1:6], refs[6:]
    outs, held_target, held, sems = refs[:-7], refs[-7], refs[-6:-1], refs[-1]
    target_copy = pltpu.make_async_copy(target_hbm, held_target, sems.at[5])
    target_copy.start()
    copies = [
        pltpu.make_async_copy(source, buffer, sems.at[index])
        for index, (source, buffer) in enumerate(zip(sources, held))
    ]
    for copy in copies:
        copy.start()
    me = lax.axis_index("req") if xor_blocks else None
    slot_total = block_count * cap_rows
    target_copy.wait()
    chosen, local = slot_one_hot(held_target[...], row_count, cap_rows, slot_total, me)
    column = 0
    for index, buffer in enumerate(held):
        copies[index].wait()
        part = buffer[...]
        if index == len(held) - 1:
            local_col = row_to_column((local + 1).astype(F32))
            labels = jnp.broadcast_to(local_col, (row_count, LANES - part.shape[1])).astype(BF16)
            part = jnp.concatenate([part, labels], axis=1)
        for begin in range(0, part.shape[1], 4 * LANES):
            piece = part[:, begin : begin + 4 * LANES]
            width = piece.shape[1]
            moved = jnp.dot(chosen, piece, preferred_element_type=F32).astype(BF16)
            for out_ref, pieces in zip(outs, layout):
                for first_block, blocks, start, end, at in pieces:
                    if start <= column < end:
                        rows = slice(first_block * cap_rows, (first_block + blocks) * cap_rows)
                        place = column - start + at
                        out_ref[:, place : place + width] = moved[rows]
            column += width


def forward(own_refs, arrived_ref, out_refs):
    width = own_refs[0].shape[1]
    for index, (own_ref, out_ref) in enumerate(zip(own_refs, out_refs)):
        out_ref[:, :width] = own_ref[...]
        out_ref[:, width:] = arrived_ref[:, (index + 1) * width : (index + 2) * width]


def joined(views, start, width):
    parts = [ref[:, start - offset : start - offset + width] for ref, offset in views]
    return parts[0] if len(parts) == 1 else jnp.concatenate(parts, axis=0)


def middle(offsets, sizes, *refs):
    query_width, keyval_width, proj_width, head_local, query_start = sizes
    blocks, refs = tuple(zip(refs, offsets)), refs[len(offsets) :]
    scalar_ref, mask_hbm, decay_hbm, bias_hbm, skip_hbm, state_hbm, cache_hbm, gain_hbm = refs[:8]
    attend_ref, weight_ref, base_ref, path_ref, kept_ref = refs[8:13]
    write_ref, order_ref, skip_out_ref, gain_ref = refs[13:17]
    mask_ref, decay_ref, bias_ref, skip_ref, state_ref, keys_ref, values_ref = refs[17:24]
    score_ref, prob_ref, rows_ref, sems = refs[24:]
    pair_heads = keyval_width // (2 * QDIM)
    cache_count = cache_hbm.shape[1]
    sources = [mask_hbm, decay_hbm, bias_hbm, skip_hbm, state_hbm, gain_hbm]
    targets = [mask_ref, decay_ref, bias_ref, skip_ref, state_ref, gain_ref]
    for pair in range(pair_heads):
        for part, held in enumerate((keys_ref, values_ref)):
            sources.append(cache_hbm.at[0, :, pl.ds((2 * pair + part) * QDIM, QDIM)])
            targets.append(held.at[pair, pl.ds(0, cache_count), pl.ds(0, QDIM)])
    loads = [
        pltpu.make_async_copy(source, held, sems.at[index])
        for index, (source, held) in enumerate(zip(sources, targets))
    ]
    for load in loads:
        load.start()
    nodes = mask_ref.shape[1]
    kv_start = query_start + query_width
    proj_start = kv_start + keyval_width
    step_start = proj_start + proj_width
    tail = joined(blocks, step_start, LANES)
    label_lane = tail[:, LANES - nodes :].astype(F32)
    slot_total = tail.shape[0]
    node_lane = lax.broadcasted_iota(jnp.int32, (slot_total, nodes), 1).astype(F32) + 1.0
    order = jnp.where(label_lane == node_lane, 1.0, 0.0).T.astype(BF16)
    order_ref[...] = order

    def ordered(start, width):
        return jnp.dot(order, joined(blocks, start, width), preferred_element_type=F32)

    length = scalar_ref[0:1, 1:2]
    key_block = 128
    for start in range(0, cache_count, key_block):
        position = lax.broadcasted_iota(jnp.int32, (key_block, LANES), 0) + start
        bias = jnp.where(position < length, 0.0, FAR).astype(BF16)
        for pair in range(pair_heads):
            keys_ref[pair, start : start + key_block, QDIM:] = bias
    for pair in range(pair_heads):
        values_ref[pair, :, QDIM:] = jnp.ones((values_ref.shape[1], LANES), BF16)

    for load in loads[:4]:
        load.wait()
    mask_float = mask_ref[0].astype(F32)
    raw = ordered(step_start, LANES)[:, :head_local] + bias_ref[...]
    step = jnp.maximum(raw, 0.0) + jnp.log1p(jnp.exp(-jnp.abs(raw)))
    cumulative = jnp.dot(
        mask_float,
        (-LOG2E * decay_ref[...]) * step,
        precision=lax.Precision.HIGHEST,
        preferred_element_type=F32,
    )
    cumulative_t = cumulative.T
    step_t = step.T
    accepted = scalar_ref[0:1, 0:1]
    node_sub = lax.broadcasted_iota(jnp.int32, (nodes, head_local), 0)
    lane_of = lax.broadcasted_iota(jnp.int32, (head_local, nodes), 1)
    pick = jnp.sum(jnp.where(node_sub == accepted, cumulative, 0.0), axis=0, keepdims=True)
    node_lanes = lax.broadcasted_iota(jnp.int32, (nodes, nodes), 1)
    mask_t = mask_float.T
    mask_pick = jnp.sum(jnp.where(node_lanes == accepted, mask_t, 0.0), axis=1, keepdims=True)
    path = mask_pick * jnp.exp2(jnp.minimum(pick - cumulative, 0.0)) * step
    pick_col = jnp.sum(jnp.where(lane_of == accepted, cumulative_t, 0.0), axis=1, keepdims=True)
    keep = jnp.broadcast_to(jnp.exp2(pick_col), (head_local, LANES))

    groups = proj_width // (2 * STATE)
    per_group = head_local // groups
    wide = LANES // HEAD_DIM
    pairs = head_local // wide
    low = lax.broadcasted_iota(jnp.int32, (pairs, LANES), 1) < HEAD_DIM
    rows_ref[0] = jnp.concatenate([cumulative_t] * wide, axis=1)
    rows_ref[1] = jnp.concatenate([step_t] * wide, axis=1)

    def pair_rows(index):
        even = rows_ref[index, pl.ds(0, pairs, stride=2), :]
        odd = rows_ref[index, pl.ds(1, pairs, stride=2), :]
        return jnp.where(low, even, odd)

    decay_pairs, step_pairs = pair_rows(0), pair_rows(1)
    columns = jnp.concatenate([cumulative, path], axis=1)
    skip_columns = jnp.broadcast_to(
        jnp.concatenate([skip_ref[...]] * wide, axis=1), (8, LANES)
    )
    half = lax.broadcasted_iota(jnp.int32, (nodes, LANES), 1) // HEAD_DIM

    def spread(table, column):
        index = half[: table.shape[0]] + column
        return jnp.take_along_axis(table, index, axis=1, mode="promise_in_bounds")

    loads[4].wait()
    for group in range(groups):
        proj = ordered(proj_start + group * 2 * STATE, 2 * STATE).astype(BF16)
        write_rows = proj[:, :STATE]
        read_rows = proj[:, STATE:]
        write_ref[:, group * STATE : (group + 1) * STATE] = write_rows
        inner = last_dot(read_rows, write_rows) * mask_float
        inner = jnp.concatenate([inner] * wide, axis=1)
        for pair in range(per_group // wide):
            head = group * per_group + pair * wide
            lanes = slice(head * HEAD_DIM, head * HEAD_DIM + LANES)
            row = slice(head // wide, head // wide + 1)
            state = state_ref[0, head : head + wide].reshape(wide * HEAD_DIM, STATE)
            carried = last_dot(read_rows, state)
            decay_i = spread(columns, head)
            weight = jnp.exp2(jnp.minimum(decay_i - decay_pairs[row], 0.0))
            weight_ref[:, lanes] = (weight * inner * step_pairs[row]).astype(BF16)
            base_ref[:, lanes] = jnp.exp2(decay_i) * carried
            path_ref[:, lanes] = spread(columns, head_local + head)
            skip_out_ref[:, lanes] = spread(skip_columns, head)[0:1]
            for index in range(head, head + wide):
                kept_ref[index] = keep[index : index + 1, :] * state_ref[0, index].astype(F32)

    group_size = query_width // QDIM // pair_heads
    scale = QDIM ** (-0.5) * LOG2E
    tree_pairs = ordered(kv_start, keyval_width).astype(BF16)
    none = jnp.zeros((keys_ref.shape[1] - cache_count - nodes, QDIM), BF16)
    tree_bias = ((1.0 - mask_t) * FAR).astype(BF16)
    tree_bias = jnp.concatenate([tree_bias, jnp.zeros_like(tree_bias)], axis=1)
    sub = lax.broadcasted_iota(jnp.int32, (nodes, LANES), 0)
    lane = lax.broadcasted_iota(jnp.int32, (nodes, LANES), 1)
    own_node = jnp.where(sub == lane, 1.0, 0.0).astype(BF16)
    tree_end = cache_count + nodes
    for pair in range(pair_heads):
        kcol = pair * 2 * QDIM
        keys_ref[pair, cache_count:tree_end, :QDIM] = tree_pairs[:, kcol : kcol + QDIM]
        keys_ref[pair, cache_count:tree_end, QDIM:] = tree_bias
        keys_ref[pair, tree_end:, :QDIM] = none
        keys_ref[pair, tree_end:, QDIM:] = jnp.full(none.shape, FAR, BF16)
        values_ref[pair, cache_count:tree_end, :QDIM] = tree_pairs[:, kcol + QDIM : kcol + 2 * QDIM]
        values_ref[pair, tree_end:, :QDIM] = none
    for load in loads[5:]:
        load.wait()
    for pair in range(pair_heads):
        first = pair * group_size * QDIM
        query = ordered(query_start + first, group_size * QDIM).astype(BF16)
        query = jnp.concatenate(
            [
                jnp.concatenate([query[:, g * QDIM : (g + 1) * QDIM], own_node], axis=1)
                for g in range(group_size)
            ],
            axis=0,
        )
        score_ref[...] = last_dot(query, keys_ref[pair])
        for start in range(0, group_size * nodes, 16):
            rows = slice(start, start + 16)
            score = score_ref[rows, :]
            peak = jnp.max(score, axis=1, keepdims=True)
            prob_ref[rows, :] = jnp.exp2((score - peak) * scale).astype(BF16)
        for g in range(0, group_size, 2):
            rows = slice(g * nodes, (g + 2) * nodes)
            result = jnp.dot(prob_ref[rows, :], values_ref[pair], preferred_element_type=F32)
            result = (result[:, :QDIM] / result[:, QDIM:]).astype(BF16)
            for part in range(2):
                column = first + (g + part) * QDIM
                attend_ref[:, column : column + QDIM] = result[part * nodes : (part + 1) * nodes]


def mix(first_offsets, second_offsets, late, *refs):
    firsts, refs = tuple(zip(refs, first_offsets)), refs[len(first_offsets) :]
    seconds, refs = tuple(zip(refs, second_offsets)), refs[len(second_offsets) :]
    order_ref, weight_ref, base_ref, skip_ref, attend_ref = refs[:5]
    mixed_ref, square_ref, input_ref, attend_hbm, sem = refs[5:]
    store = pltpu.make_async_copy(attend_ref, attend_hbm, sem)
    store.start()
    nodes, width = base_ref.shape
    order = order_ref[...]
    sub = lax.broadcasted_iota(jnp.int32, (2 * nodes, LANES), 0) < nodes
    lane = lax.broadcasted_iota(jnp.int32, (2 * nodes, LANES), 1) < HEAD_DIM
    same = sub == lane
    total = jnp.zeros((nodes, LANES), F32)
    chunk = 4 * LANES

    def ordered(start):
        views = seconds if start < late else firsts
        return jnp.dot(order, joined(views, start, chunk), preferred_element_type=F32)

    ahead = ordered(0)
    for start in range(0, width, chunk):
        wide = ahead
        if start + chunk < width:
            ahead = ordered(start + chunk)
        rows = wide.astype(BF16)
        input_ref[:, start : start + chunk] = rows
        for begin in range(0, chunk, LANES):
            lanes = slice(start + begin, start + begin + LANES)
            one = rows[:, begin : begin + LANES]
            both = jnp.concatenate([one, one], axis=0)
            both = jnp.where(same, both, jnp.zeros_like(both))
            mixed = jnp.dot(weight_ref[:, lanes], both, preferred_element_type=F32)
            mixed = mixed + base_ref[:, lanes] + skip_ref[:, lanes] * wide[:, begin : begin + LANES]
            mixed_ref[:, lanes] = mixed
            total = total + mixed * mixed
    square_ref[...] = jnp.broadcast_to(jnp.sum(total, axis=1, keepdims=True), square_ref.shape)
    store.wait()


def advance(input_ref, path_ref, write_ref, kept_ref, out_ref):
    head_local = kept_ref.shape[0]
    groups = write_ref.shape[1] // STATE
    per_group = head_local // groups
    width = per_group * HEAD_DIM
    for group in range(groups):
        lanes = slice(group * width, (group + 1) * width)
        weighted = (path_ref[:, lanes] * input_ref[:, lanes].astype(F32)).astype(BF16)
        update = lax.dot_general(
            weighted,
            write_ref[:, group * STATE : (group + 1) * STATE],
            (((0,), (0,)), ((), ())),
            preferred_element_type=F32,
        )
        for index in range(per_group):
            head = group * per_group + index
            out_ref[0, head] = (
                kept_ref[head] + update[index * HEAD_DIM : (index + 1) * HEAD_DIM]
            ).astype(BF16)


def finish(total_width, mixed_ref, mine_ref, other_ref, gain_ref, state_ref, *refs):
    out_hbm, state_hbm, out_ref, sems = refs
    chunks = sems.shape[0] - 1
    store = pltpu.make_async_copy(state_ref, state_hbm, sems.at[chunks])
    store.start()
    square = mine_ref[...] + other_ref[...]
    scale = 1.0 / jnp.sqrt(square / total_width + 1e-05)
    width = out_ref.shape[1] // chunks
    stores = [store]
    for chunk in range(chunks):
        for start in range(chunk * width, (chunk + 1) * width, LANES):
            lanes = slice(start, start + LANES)
            out_ref[:, lanes] = (mixed_ref[:, lanes] * scale * gain_ref[:, lanes]).astype(BF16)
        view = pl.ds(chunk * width, width)
        stores.append(
            pltpu.make_async_copy(out_ref.at[:, view], out_hbm.at[:, view], sems.at[chunk])
        )
        stores[-1].start()
    for store in stores:
        store.wait()


SPACES = {"h": pltpu.HBM, "v": pltpu.VMEM, "s": pltpu.SMEM}


def call(body, ins, outs, scratch=(), mebibytes=8):
    def run(*operands):
        placed = [
            operand if space == "s" else pltpu.with_memory_space_constraint(operand, SPACES[space])
            for space, operand in zip(ins, operands, strict=True)
        ]
        return pl.pallas_call(
            body,
            out_shape=tuple(SPACES[space](dims, kind) for space, dims, kind in outs),
            in_specs=[pl.BlockSpec(memory_space=SPACES[space]) for space in ins],
            out_specs=tuple(pl.BlockSpec(memory_space=SPACES[out[0]]) for out in outs),
            scratch_shapes=scratch,
            compiler_params=pltpu.CompilerParams(vmem_limit_bytes=mebibytes * 1024 * 1024),
        )(*placed)

    return run


def local(
    draft_input,
    draft_proj,
    draft_step,
    draft_query,
    draft_keyval,
    row_target,
    tree_mask,
    accepted,
    cache_length,
    scan_state,
    cache_keyval,
    decay_rate,
    step_bias,
    skip_gain,
    norm_gain,
):
    row_count, scan_width = draft_input.shape
    peers = lax.axis_size("req")
    head_shards = lax.axis_size("head")
    cap_rows = max(2, row_count // peers)
    slot_total = peers * cap_rows
    direct = 4 <= peers <= 16 and peers & (peers - 1) == 0
    head_local = scan_width // HEAD_DIM
    query_width = draft_query.shape[1]
    keyval_width = draft_keyval.shape[1]
    proj_width = draft_proj.shape[1]
    groups = proj_width // (2 * STATE)
    all_width = scan_width + query_width + keyval_width + proj_width + LANES
    early = int(EARLY * scan_width) if direct else scan_width
    late = scan_width - early
    rest_width = all_width - late
    if direct:
        odd = range(1, peers, 2)
        even = range(2, peers, 2)
        layout = [((0, 1, 0, all_width, 0),)]
        layout += [((block, 1, late, all_width, 0),) for block in range(1, peers)]
        layout += [((block, 1, 0, late, 0),) for block in even]
        layout += [tuple((block, 1, 0, late, index * late) for index, block in enumerate(odd))]
        widths = [all_width] + [rest_width] * (peers - 1)
        widths += [late] * len(even) + [late * len(odd)]
        rows_of = cap_rows
    else:
        layout, widths = [((0, peers, 0, all_width, 0),)], [all_width]
        rows_of = slot_total
    sources = (draft_input, draft_query, draft_keyval, draft_proj, draft_step)
    packed = call(
        functools.partial(pack, (row_count, cap_rows, peers), direct, layout),
        "h" * 6,
        tuple(("v", (rows_of, width), BF16) for width in widths),
        scratch=[pltpu.VMEM((1, row_count), jnp.int32)]
        + [pltpu.VMEM(source.shape, BF16) for source in sources]
        + [pltpu.SemaphoreType.DMA((6,))],
    )(row_target.reshape(1, row_count), *sources)

    def moved(block, step):
        pairs = [(index, index ^ step) for index in range(peers)]
        return lax.ppermute(block, "req", pairs)

    if direct:
        own, rest, inputs = packed[0], packed[1:peers], packed[peers:]
        arrived = moved(inputs[-1], 1)
        rest = [moved(block, step) for step, block in enumerate(rest, start=1)]
        count = len(even)

        def forward_all(*refs):
            forward(refs[:count], refs[count], refs[count + 1 :])

        pairs = call(
            forward_all, "v" * (count + 1), (("v", (cap_rows, 2 * late), BF16),) * count
        )(*inputs[:-1], arrived)
        pairs = [moved(block, step) for step, block in zip(even, pairs)]
        first_blocks, first_offsets = [own] + rest, [0] + [late] * (peers - 1)
        second_blocks, second_offsets = [own, arrived], [0, 0]
        for block in pairs:
            second_blocks += [block, block]
            second_offsets += [0, -late]
    else:
        split = packed[0].reshape(peers, cap_rows, all_width)
        arrived = lax.all_to_all(split, "req", split_axis=0, concat_axis=0, tiled=True)
        first_blocks, first_offsets = [arrived.reshape(slot_total, all_width)], [0]
        second_blocks, second_offsets = [], []

    scalars = lax.pad(accepted, 0, [(0, LANES - 1, 0)]) + lax.pad(
        cache_length, 0, [(1, LANES - 2, 0)]
    )
    scalars = scalars.reshape(1, LANES)
    pair_heads = keyval_width // (2 * QDIM)
    score_rows = NODES * (query_width // QDIM // pair_heads)
    key_rows = cache_keyval.shape[1] + LANES
    attended, weight, base, path, kept, write, order, skip_wide, gain = call(
        functools.partial(
            middle,
            first_offsets,
            (query_width, keyval_width, proj_width, head_local, scan_width),
        ),
        "v" * (len(first_blocks) + 1) + "h" * 7,
        (
            ("v", (row_count, query_width), BF16),
            ("v", (NODES, head_local * NODES), BF16),
            ("v", (NODES, scan_width), F32),
            ("v", (NODES, scan_width), F32),
            ("v", (head_local, HEAD_DIM, STATE), F32),
            ("v", (NODES, groups * STATE), BF16),
            ("v", (NODES, slot_total), BF16),
            ("v", (1, scan_width), F32),
            ("v", (1, scan_width), F32),
        ),
        scratch=[
            pltpu.VMEM(tree_mask.shape, jnp.int32),
            pltpu.VMEM((1, head_local), F32),
            pltpu.VMEM((1, head_local), F32),
            pltpu.VMEM((1, head_local), F32),
            pltpu.VMEM(scan_state.shape, BF16),
            pltpu.VMEM((pair_heads, key_rows, 2 * QDIM), BF16),
            pltpu.VMEM((pair_heads, key_rows, 2 * QDIM), BF16),
            pltpu.VMEM((score_rows, key_rows), F32),
            pltpu.VMEM((score_rows, key_rows), BF16),
            pltpu.VMEM((2, head_local, LANES), F32),
            pltpu.SemaphoreType.DMA((6 + 2 * pair_heads,)),
        ],
        mebibytes=24,
    )(
        *first_blocks,
        scalars,
        tree_mask,
        decay_rate.reshape(1, head_local),
        step_bias.reshape(1, head_local),
        skip_gain.reshape(1, head_local),
        scan_state,
        cache_keyval,
        norm_gain.reshape(1, scan_width),
    )

    mixed, square, inputs, attend_out = call(
        functools.partial(mix, first_offsets, second_offsets, late),
        "v" * (len(first_blocks) + len(second_blocks) + 5),
        (
            ("v", (NODES, scan_width), F32),
            ("v", (NODES, LANES), F32),
            ("v", (NODES, scan_width), BF16),
            ("h", (row_count, query_width), BF16),
        ),
        scratch=[pltpu.SemaphoreType.DMA(())],
    )(*first_blocks, *second_blocks, order, weight, base, skip_wide, attended)
    swap = [(index, (index + 1) % head_shards) for index in range(head_shards)]
    other = lax.ppermute(square, "head", swap)
    new_state = call(advance, "v" * 4, (("v", scan_state.shape, BF16),))(
        inputs, path, write, kept
    )[0]
    mixer_out, new_state = call(
        functools.partial(finish, head_shards * scan_width),
        "v" * 5,
        (("h", (row_count, scan_width), BF16), ("h", scan_state.shape, BF16)),
        scratch=[pltpu.VMEM((row_count, scan_width), BF16), pltpu.SemaphoreType.DMA((5,))],
    )(mixed, square, other, gain, new_state)
    return (mixer_out, attend_out, new_state)


def solution(mesh):
    assert mesh.shape["head"] == 2
    rows = P(("grp", "req"), "head")

    return jax.shard_map(
        local,
        mesh=mesh,
        in_specs=(
            rows,
            rows,
            rows,
            rows,
            rows,
            P(("grp", "req")),
            P(("grp", "req"), None, None),
            P(("grp", "req")),
            P(("grp", "req")),
            P(("grp", "req"), "head", None, None),
            P(("grp", "req"), None, "head"),
            P("head"),
            P("head"),
            P("head"),
            P("head"),
        ),
        out_specs=(rows, rows, P(("grp", "req"), "head", None, None)),
        check_vma=False,
    )
```

time: 39.1 us -> 44.3 us (1.13)
  the two profiles are of different devices: /device:TPU:0 before, /device:TPU:13 now
where the time goes in v1:
time: 44.3 us; the launch traced here: 44.2 us
  waiting for transfers between devices  16.2 us (37%)
  starting transfers between devices  15.7 us (35%)
  Pallas kernels  10.2 us (23%)
  between operations  2.04 us (5%)
    ppermute x11, waiting for transfers between devices, moved(): return lax.ppermute(block, 'req', pairs)  15.9 us
    ppermute x11, starting transfers between devices, moved(): return lax.ppermute(block, 'req', pairs)  13.6 us
    pallas_call x6, Pallas kernels, run(): pl.pallas_call(body, out_shape=tuple((SPACES[space](dims, kind) for space...  10.2 us
    ppermute x1, starting transfers between devices, local(): other = lax.ppermute(square, 'head', swap)  2.04 us
  transfers between devices with their start and end apart: 12, of which 4 were waited for; matrix products, arithmetic and copies ran while one was open for 0% of the time, Pallas kernels for 13%

profile of v1, /device:TPU:13, one launch (start us, length us, event | category | flops | bytes accessed | tf_op | source)
XLA Modules:
  0.0 44.2 jit_solution(9205022780661134327)
XLA Ops:
  0.6 2.1 %shard_map.166 = (bf16[8,7808]{1,0:T(8,128)(2,1)S(1)}, bf16[8,3712]{1,0:T(8,128)(2,1)S(1)}, bf16[8,3712]{1,0:T(8,128)(2,1)S(1)}, bf16[8,3712]{1,0:T(8,128)(2,1)S...) custom-call(s32[1,64]{1,0:T(1,128)} %bitcast.8, ...), custom_call_target="tpu_custom_call" | custom-call | tf_op jit(solution)/shard_map/pallas_call | solution.py:354
  2.8 1.3 %collective-permute-start.7 = (bf16[8,16384]{1,0:T(8,128)(2,1)S(1)}, bf16[8,16384]{1,0:T(8,128)(2,1)S(1)}, u32[]{:S(2)}, u32[]{:S(2)}) collective-permute-start(bf16[8,16384]{1,0:T(8,128)(2,1)S(1)} %get-tuple-element.41), channel_id=1, source_target_pairs={{0,2},{2,0},{4,6},{6,4},{8,10},{10,8},{12,14},{14,12},{1,3},{3,1},... | collective-permute-start | bytes 786440 | tf_op jit(solution)/shard_map/ppermute | solution.py:423
  4.0 0.2 collective-permute-start
  4.3 0.2 collective-permute-start.1
  4.5 2.2 %collective-permute-start.2 = (bf16[8,3712]{1,0:T(8,128)(2,1)S(1)}, bf16[8,3712]{1,0:T(8,128)(2,1)S(1)}, u32[]{:S(2)}, u32[]{:S(2)}) collective-permute-start(bf16[8,3712]{1,0:T(8,128)(2,1)S(1)} %get-tuple-element.36), channel_id=1, source_target_pairs={{0,6},{2,4},{4,2},{6,0},{8,14},{10,12},{12,10},{14,8},{1,7},{3,5},... | collective-permute-start | bytes 178184 | tf_op jit(solution)/shard_map/ppermute | solution.py:423
  6.7 2.3 %collective-permute-start.3 = (bf16[8,3712]{1,0:T(8,128)(2,1)S(1)}, bf16[8,3712]{1,0:T(8,128)(2,1)S(1)}, u32[]{:S(2)}, u32[]{:S(2)}) collective-permute-start(bf16[8,3712]{1,0:T(8,128)(2,1)S(1)} %get-tuple-element.37), channel_id=1, source_target_pairs={{0,8},{2,10},{4,12},{6,14},{8,0},{10,2},{12,4},{14,6},{1,9},{3,11}... | collective-permute-start | bytes 178184 | tf_op jit(solution)/shard_map/ppermute | solution.py:423
  9.0 2.1 %collective-permute-done.7.refs_3_.refs_9_ = bf16[8,16384]{1,0:T(8,128)(2,1)S(1)} collective-permute-done((bf16[8,16384]{1,0:T(8,128)(2,1)S(1)}, bf16[8,16384]{1,0:T(8,128)(2,1)S(1)}, u32[]{:S(2)}, u32[]{:S(2)}) %collective-permute-start.7) | collective-permute-done | bytes 262176 | tf_op jit(solution)/shard_map/ppermute | solution.py:423
  11.1 3.4 %collective-permute-start.4 = (bf16[8,3712]{1,0:T(8,128)(2,1)S(1)}, bf16[8,3712]{1,0:T(8,128)(2,1)S(1)}, u32[]{:S(2)}, u32[]{:S(2)}) collective-permute-start(bf16[8,3712]{1,0:T(8,128)(2,1)S(1)} %get-tuple-element.38), channel_id=1, source_target_pairs={{0,10},{2,8},{4,14},{6,12},{8,2},{10,0},{12,6},{14,4},{1,11},{3,9}... | collective-permute-start | bytes 178184 | tf_op jit(solution)/shard_map/ppermute | solution.py:423
  14.6 0.0 collective-permute-done.refs_1_
  14.6 0.1 collective-permute-start.8
  14.6 0.0 collective-permute-done.1.refs_2_
  14.7 0.4 collective-permute-start.9
  15.0 0.0 collective-permute-done.2.refs_3_
  15.0 2.2 %collective-permute-start.10 = (bf16[8,8192]{1,0:T(8,128)(2,1)S(1)}, bf16[8,8192]{1,0:T(8,128)(2,1)S(1)}, u32[]{:S(2)}, u32[]{:S(2)}) collective-permute-start(bf16[8,8192]{1,0:T(8,128)(2,1)S(1)} %get-tuple-element.47), channel_id=1, source_target_pairs={{0,12},{2,14},{4,8},{6,10},{8,4},{10,6},{12,0},{14,2},{1,13},{3,15... | collective-permute-start | bytes 393224 | tf_op jit(solution)/shard_map/ppermute | solution.py:423
  18.6 0.0 collective-permute-done.3.refs_4_
  18.6 0.1 collective-permute-start.5
  18.7 0.0 collective-permute-done.4.refs_5_
  18.7 1.2 %collective-permute-start.6 = (bf16[8,3712]{1,0:T(8,128)(2,1)S(1)}, bf16[8,3712]{1,0:T(8,128)(2,1)S(1)}, u32[]{:S(2)}, u32[]{:S(2)}) collective-permute-start(bf16[8,3712]{1,0:T(8,128)(2,1)S(1)} %get-tuple-element.40), channel_id=1, source_target_pairs={{0,14},{2,12},{4,10},{6,8},{8,6},{10,4},{12,2},{14,0},{1,15},{3,13... | collective-permute-start | bytes 178184 | tf_op jit(solution)/shard_map/ppermute | solution.py:423
  19.9 0.1 add_bitcast_fusion.refs_8_
  20.0 13.0 %collective-permute-done.5.refs_6_ = bf16[8,3712]{1,0:T(8,128)(2,1)S(1)} collective-permute-done((bf16[8,3712]{1,0:T(8,128)(2,1)S(1)}, bf16[8,3712]{1,0:T(8,128)(2,1)S(1)}, u32[]{:S(2)}, u32[]{:S(2)}) %collective-permute-start.5) | collective-permute-done | bytes 59424 | tf_op jit(solution)/shard_map/ppermute | solution.py:423
  33.0 0.7 %collective-permute-done.6.refs_7_ = bf16[8,3712]{1,0:T(8,128)(2,1)S(1)} collective-permute-done((bf16[8,3712]{1,0:T(8,128)(2,1)S(1)}, bf16[8,3712]{1,0:T(8,128)(2,1)S(1)}, u32[]{:S(2)}, u32[]{:S(2)}) %collective-permute-start.6) | collective-permute-done | bytes 59424 | tf_op jit(solution)/shard_map/ppermute | solution.py:423
  33.7 5.3 %shard_map.168 = (bf16[64,2048]{1,0:T(8,128)(2,1)S(1)}, bf16[64,4096]{1,0:T(8,128)(2,1)S(1)}, f32[64,4096]{1,0:T(8,128)S(1)}, f32[64,4096]{1,0:T(8,128)S(1)}, f3...) custom-call(bf16[8,7808]{1,0:T(8,128)(2,1)S(1)} %get-tuple-element.3, ...), custom_call_target="tpu_custom_call" | custom-call | tf_op jit(solution)/shard_map/pallas_call | solution.py:354
  39.0 0.0 collective-permute-done.8.refs_10_.refs_11_
  39.0 0.0 collective-permute-done.9.refs_12_.refs_13_
  39.0 0.0 collective-permute-done.10.refs_14_.refs_15_
  39.0 1.1 %shard_map.169 = (f32[64,4096]{1,0:T(8,128)S(1)}, f32[64,128]{1,0:T(8,128)S(1)}, bf16[64,4096]{1,0:T(8,128)(2,1)S(1)}, bf16[64,2048]{1,0:T(8,128)(2,1)}) custom-call(bf16[8,7808]{1,0:T(8,128)(2,1)S(1)} %get-tuple-element.33.refs_0_.refs_8_, bf16[8,3712]{1,0:T(8,128)(2,1)S(1)} %collective-permute-done.refs_1_, ...), custom_call_target="tpu_custom_call" | custom-call | tf_op jit(solution)/shard_map/pallas_call | solution.py:354
  40.1 2.0 %collective-permute-start.11 = (f32[64,128]{1,0:T(8,128)S(1)}, f32[64,128]{1,0:T(8,128)S(1)}, u32[]{:S(2)}, u32[]{:S(2)}) collective-permute-start(f32[64,128]{1,0:T(8,128)S(1)} %get-tuple-element.54.mine_ref), channel_id=1, source_target_pairs={{0,1},{1,0},{2,3},{3,2},{4,5},{5,4},{6,7},{7,6},{8,9},{9,8},{10,11... | collective-permute-start | bytes 98312 | tf_op jit(solution)/shard_map/ppermute | solution.py:512
  42.1 0.5 %shard_map.170.state_ref = bf16[1,64,64,128]{3,2,1,0:T(8,128)(2,1)S(1)} custom-call(bf16[64,4096]{1,0:T(8,128)(2,1)S(1)} %get-tuple-element.56.input_ref, f32[64,4096]{1,0:T(8,128)S(1)} %get-tuple-element.57.path_ref, bf16[64,512]{1,0:T(8,128)(2,1)S(1)} %get-tuple-element.58.write_ref, f32[64,64,128]{2,1,0:T(8,128)S(1)} %get-tuple-element.59.kept_ref), custom_call_target="tpu_custom_call" | custom-call | tf_op jit(solution)/shard_map/pallas_call | solution.py:354
  42.7 0.3 collective-permute-done.11.other_ref
  43.0 1.2 %shard_map.171 = (bf16[64,4096]{1,0:T(8,128)(2,1)}, bf16[1,64,64,128]{3,2,1,0:T(8,128)(2,1)}) custom-call(f32[64,4096]{1,0:T(8,128)S(1)} %get-tuple-element.53.mixed_ref, f32[64,128]{1,0:T(8,128)S(1)} %get-tuple-element.54.mine_ref, f32[64,128]{1,0:T(8,128)S(1)} %collective-permute-done.11.other_ref, f32[1,4096]{1,0:T(1,128)S(1)} %get-tuple-element.55.gain_ref, ...), custom_call_target="tpu_custom_call" | custom-call | tf_op jit(solution)/shard_map/pallas_call | solution.py:354
  (1 shorter events, 0.0 us)
Async XLA Ops:
  2.8 8.4 %collective-permute-start.7 = (bf16[8,16384]{1,0:T(8,128)(2,1)S(1)}, bf16[8,16384]{1,0:T(8,128)(2,1)S(1)}, u32[]{:S(2)}, u32[]{:S(2)}) collective-permute-start(bf16[8,16384]{1,0:T(8,128)(2,1)S(1)} %get-tuple-element.41), channel_id=1, source_target_pairs={{0,2},{2,0},{4,6},{6,4},{8,10},{10,8},{12,14},{14,12},{1,3},{3,1},... | collective-permute-start | bytes 786440 | tf_op jit(solution)/shard_map/ppermute | solution.py:423
  4.0 10.5 %collective-permute-start = (bf16[8,3712]{1,0:T(8,128)(2,1)S(1)}, bf16[8,3712]{1,0:T(8,128)(2,1)S(1)}, u32[]{:S(2)}, u32[]{:S(2)}) collective-permute-start(bf16[8,3712]{1,0:T(8,128)(2,1)S(1)} %get-tuple-element.34), channel_id=1, source_target_pairs={{0,2},{2,0},{4,6},{6,4},{8,10},{10,8},{12,14},{14,12},{1,3},{3,1},... | collective-permute-start | bytes 178184 | tf_op jit(solution)/shard_map/ppermute | solution.py:423
  4.3 10.4 %collective-permute-start.1 = (bf16[8,3712]{1,0:T(8,128)(2,1)S(1)}, bf16[8,3712]{1,0:T(8,128)(2,1)S(1)}, u32[]{:S(2)}, u32[]{:S(2)}) collective-permute-start(bf16[8,3712]{1,0:T(8,128)(2,1)S(1)} %get-tuple-element.35), channel_id=1, source_target_pairs={{0,4},{2,6},{4,0},{6,2},{8,12},{10,14},{12,8},{14,10},{1,5},{3,7},... | collective-permute-start | bytes 178184 | tf_op jit(solution)/shard_map/ppermute | solution.py:423
  4.5 10.6 %collective-permute-start.2 = (bf16[8,3712]{1,0:T(8,128)(2,1)S(1)}, bf16[8,3712]{1,0:T(8,128)(2,1)S(1)}, u32[]{:S(2)}, u32[]{:S(2)}) collective-permute-start(bf16[8,3712]{1,0:T(8,128)(2,1)S(1)} %get-tuple-element.36), channel_id=1, source_target_pairs={{0,6},{2,4},{4,2},{6,0},{8,14},{10,12},{12,10},{14,8},{1,7},{3,5},... | collective-permute-start | bytes 178184 | tf_op jit(solution)/shard_map/ppermute | solution.py:423
  6.7 11.9 %collective-permute-start.3 = (bf16[8,3712]{1,0:T(8,128)(2,1)S(1)}, bf16[8,3712]{1,0:T(8,128)(2,1)S(1)}, u32[]{:S(2)}, u32[]{:S(2)}) collective-permute-start(bf16[8,3712]{1,0:T(8,128)(2,1)S(1)} %get-tuple-element.37), channel_id=1, source_target_pairs={{0,8},{2,10},{4,12},{6,14},{8,0},{10,2},{12,4},{14,6},{1,9},{3,11}... | collective-permute-start | bytes 178184 | tf_op jit(solution)/shard_map/ppermute | solution.py:423
  11.1 7.5 %collective-permute-start.4 = (bf16[8,3712]{1,0:T(8,128)(2,1)S(1)}, bf16[8,3712]{1,0:T(8,128)(2,1)S(1)}, u32[]{:S(2)}, u32[]{:S(2)}) collective-permute-start(bf16[8,3712]{1,0:T(8,128)(2,1)S(1)} %get-tuple-element.38), channel_id=1, source_target_pairs={{0,10},{2,8},{4,14},{6,12},{8,2},{10,0},{12,6},{14,4},{1,11},{3,9}... | collective-permute-start | bytes 178184 | tf_op jit(solution)/shard_map/ppermute | solution.py:423
  14.6 24.4 %collective-permute-start.8 = (bf16[8,8192]{1,0:T(8,128)(2,1)S(1)}, bf16[8,8192]{1,0:T(8,128)(2,1)S(1)}, u32[]{:S(2)}, u32[]{:S(2)}) collective-permute-start(bf16[8,8192]{1,0:T(8,128)(2,1)S(1)} %get-tuple-element.45), channel_id=1, source_target_pairs={{0,4},{2,6},{4,0},{6,2},{8,12},{10,14},{12,8},{14,10},{1,5},{3,7},... | collective-permute-start | bytes 393224 | tf_op jit(solution)/shard_map/ppermute | solution.py:423
  14.7 24.4 %collective-permute-start.9 = (bf16[8,8192]{1,0:T(8,128)(2,1)S(1)}, bf16[8,8192]{1,0:T(8,128)(2,1)S(1)}, u32[]{:S(2)}, u32[]{:S(2)}) collective-permute-start(bf16[8,8192]{1,0:T(8,128)(2,1)S(1)} %get-tuple-element.46), channel_id=1, source_target_pairs={{0,8},{2,10},{4,12},{6,14},{8,0},{10,2},{12,4},{14,6},{1,9},{3,11}... | collective-permute-start | bytes 393224 | tf_op jit(solution)/shard_map/ppermute | solution.py:423
  15.0 24.0 %collective-permute-start.10 = (bf16[8,8192]{1,0:T(8,128)(2,1)S(1)}, bf16[8,8192]{1,0:T(8,128)(2,1)S(1)}, u32[]{:S(2)}, u32[]{:S(2)}) collective-permute-start(bf16[8,8192]{1,0:T(8,128)(2,1)S(1)} %get-tuple-element.47), channel_id=1, source_target_pairs={{0,12},{2,14},{4,8},{6,10},{8,4},{10,6},{12,0},{14,2},{1,13},{3,15... | collective-permute-start | bytes 393224 | tf_op jit(solution)/shard_map/ppermute | solution.py:423
  18.6 14.4 %collective-permute-start.5 = (bf16[8,3712]{1,0:T(8,128)(2,1)S(1)}, bf16[8,3712]{1,0:T(8,128)(2,1)S(1)}, u32[]{:S(2)}, u32[]{:S(2)}) collective-permute-start(bf16[8,3712]{1,0:T(8,128)(2,1)S(1)} %get-tuple-element.39), channel_id=1, source_target_pairs={{0,12},{2,14},{4,8},{6,10},{8,4},{10,6},{12,0},{14,2},{1,13},{3,15... | collective-permute-start | bytes 178184 | tf_op jit(solution)/shard_map/ppermute | solution.py:423
  18.7 15.0 %collective-permute-start.6 = (bf16[8,3712]{1,0:T(8,128)(2,1)S(1)}, bf16[8,3712]{1,0:T(8,128)(2,1)S(1)}, u32[]{:S(2)}, u32[]{:S(2)}) collective-permute-start(bf16[8,3712]{1,0:T(8,128)(2,1)S(1)} %get-tuple-element.40), channel_id=1, source_target_pairs={{0,14},{2,12},{4,10},{6,8},{8,6},{10,4},{12,2},{14,0},{1,15},{3,13... | collective-permute-start | bytes 178184 | tf_op jit(solution)/shard_map/ppermute | solution.py:423
  40.1 2.9 %collective-permute-start.11 = (f32[64,128]{1,0:T(8,128)S(1)}, f32[64,128]{1,0:T(8,128)S(1)}, u32[]{:S(2)}, u32[]{:S(2)}) collective-permute-start(f32[64,128]{1,0:T(8,128)S(1)} %get-tuple-element.54.mine_ref), channel_id=1, source_target_pairs={{0,1},{1,0},{2,3},{3,2},{4,5},{5,4},{6,7},{7,6},{8,9},{9,8},{10,11... | collective-permute-start | bytes 98312 | tf_op jit(solution)/shard_map/ppermute | solution.py:512

commit v2 on v1

--- a/solution.py
+++ b/solution.py
@@ -15,7 +15,11 @@
 LANES = 128
 LOG2E = 1.4426950408889634
 FAR = -1e30
-EARLY = 0.0
+EARLY_FROM = (8, 8, 8, 8, 0, 8, 8, 8)
+SCORE_EVERY = 1
+SOFT_FROM = 12
+SOFT_EACH = 2
+ATTEND_PARTS = 4
 F32 = jnp.float32
 BF16 = jnp.bfloat16
 
@@ -59,16 +63,19 @@
         pltpu.make_async_copy(source, buffer, sems.at[index])
         for index, (source, buffer) in enumerate(zip(sources, held))
     ]
-    for copy in copies:
+    for copy in copies[1:] + copies[:1]:
         copy.start()
     me = lax.axis_index("req") if xor_blocks else None
     slot_total = block_count * cap_rows
     target_copy.wait()
     chosen, local = slot_one_hot(held_target[...], row_count, cap_rows, slot_total, me)
-    column = 0
-    for index, buffer in enumerate(held):
+    columns = [0]
+    for buffer in held:
+        columns.append(columns[-1] + buffer.shape[1])
+    for index in list(range(1, len(held))) + [0]:
         copies[index].wait()
-        part = buffer[...]
+        part = held[index][...]
+        column = columns[index]
         if index == len(held) - 1:
             local_col = row_to_column((local + 1).astype(F32))
             labels = jnp.broadcast_to(local_col, (row_count, LANES - part.shape[1])).astype(BF16)
@@ -86,34 +93,42 @@
             column += width
 
 
-def forward(own_refs, arrived_ref, out_refs):
-    width = own_refs[0].shape[1]
-    for index, (own_ref, out_ref) in enumerate(zip(own_refs, out_refs)):
-        out_ref[:, :width] = own_ref[...]
-        out_ref[:, width:] = arrived_ref[:, (index + 1) * width : (index + 2) * width]
+def forward(widths, arrived_ref, starts, own_refs, out_refs):
+    for (own, more), start, own_ref, out_ref in zip(widths, starts, own_refs, out_refs):
+        if own:
+            out_ref[:, :own] = own_ref[:, :own]
+        if more:
+            out_ref[:, own:] = arrived_ref[:, start : start + more]
 
 
 def joined(views, start, width):
     parts = [ref[:, start - offset : start - offset + width] for ref, offset in views]
     return parts[0] if len(parts) == 1 else jnp.concatenate(parts, axis=0)
+
+
+def spread(table, column):
+    half = lax.broadcasted_iota(jnp.int32, table.shape, 1) // HEAD_DIM
+    return jnp.take_along_axis(table, half + column, axis=1, mode="promise_in_bounds")
 
 
 def middle(offsets, sizes, *refs):
     query_width, keyval_width, proj_width, head_local, query_start = sizes
     blocks, refs = tuple(zip(refs, offsets)), refs[len(offsets) :]
     scalar_ref, mask_hbm, decay_hbm, bias_hbm, skip_hbm, state_hbm, cache_hbm, gain_hbm = refs[:8]
-    attend_ref, weight_ref, base_ref, path_ref, kept_ref = refs[8:13]
+    attend_ref, weight_ref, base_ref, columns_ref, keep_ref = refs[8:13]
     write_ref, order_ref, skip_out_ref, gain_ref = refs[13:17]
-    mask_ref, decay_ref, bias_ref, skip_ref, state_ref, keys_ref, values_ref = refs[17:24]
-    score_ref, prob_ref, rows_ref, sems = refs[24:]
+    state_ref, mask_ref, decay_ref, bias_ref, skip_ref, keys_ref, values_ref = refs[17:24]
+    query_ref, score_ref, prob_ref, rows_ref, sems = refs[24:]
     pair_heads = keyval_width // (2 * QDIM)
     cache_count = cache_hbm.shape[1]
-    sources = [mask_hbm, decay_hbm, bias_hbm, skip_hbm, state_hbm, gain_hbm]
-    targets = [mask_ref, decay_ref, bias_ref, skip_ref, state_ref, gain_ref]
+    sources = [mask_hbm, decay_hbm, bias_hbm, skip_hbm]
+    targets = [mask_ref, decay_ref, bias_ref, skip_ref]
     for pair in range(pair_heads):
         for part, held in enumerate((keys_ref, values_ref)):
             sources.append(cache_hbm.at[0, :, pl.ds((2 * pair + part) * QDIM, QDIM)])
             targets.append(held.at[pair, pl.ds(0, cache_count), pl.ds(0, QDIM)])
+    sources += [state_hbm, gain_hbm]
+    targets += [state_ref, gain_ref]
     loads = [
         pltpu.make_async_copy(source, held, sems.at[index])
         for index, (source, held) in enumerate(zip(sources, targets))
@@ -135,12 +150,8 @@
         return jnp.dot(order, joined(blocks, start, width), preferred_element_type=F32)
 
     length = scalar_ref[0:1, 1:2]
-    key_block = 128
-    for start in range(0, cache_count, key_block):
-        position = lax.broadcasted_iota(jnp.int32, (key_block, LANES), 0) + start
-        bias = jnp.where(position < length, 0.0, FAR).astype(BF16)
-        for pair in range(pair_heads):
-            keys_ref[pair, start : start + key_block, QDIM:] = bias
+    position = lax.broadcasted_iota(jnp.int32, (1, cache_count), 1)
+    cache_bias = jnp.where(position < length, 0.0, FAR)
     for pair in range(pair_heads):
         values_ref[pair, :, QDIM:] = jnp.ones((values_ref.shape[1], LANES), BF16)
 
@@ -166,7 +177,7 @@
     mask_pick = jnp.sum(jnp.where(node_lanes == accepted, mask_t, 0.0), axis=1, keepdims=True)
     path = mask_pick * jnp.exp2(jnp.minimum(pick - cumulative, 0.0)) * step
     pick_col = jnp.sum(jnp.where(lane_of == accepted, cumulative_t, 0.0), axis=1, keepdims=True)
-    keep = jnp.broadcast_to(jnp.exp2(pick_col), (head_local, LANES))
+    keep_ref[...] = jnp.broadcast_to(jnp.exp2(pick_col), (head_local, LANES))
 
     groups = proj_width // (2 * STATE)
     per_group = head_local // groups
@@ -183,16 +194,60 @@
 
     decay_pairs, step_pairs = pair_rows(0), pair_rows(1)
     columns = jnp.concatenate([cumulative, path], axis=1)
+    columns_ref[...] = columns
     skip_columns = jnp.broadcast_to(
         jnp.concatenate([skip_ref[...]] * wide, axis=1), (8, LANES)
     )
-    half = lax.broadcasted_iota(jnp.int32, (nodes, LANES), 1) // HEAD_DIM
-
-    def spread(table, column):
-        index = half[: table.shape[0]] + column
-        return jnp.take_along_axis(table, index, axis=1, mode="promise_in_bounds")
-
-    loads[4].wait()
+    group_size = query_width // QDIM // pair_heads
+    scale = QDIM ** (-0.5) * LOG2E
+    tree_pairs = ordered(kv_start, keyval_width).astype(BF16)
+    none = jnp.zeros((keys_ref.shape[1] - cache_count - nodes, QDIM), BF16)
+    tree_bias = (1.0 - mask_float) * FAR
+    past = jnp.full((nodes, keys_ref.shape[1] - cache_count - nodes), FAR, F32)
+    tree_bias = jnp.concatenate([tree_bias, past], axis=1)
+    tree_end = cache_count + nodes
+    for pair in range(pair_heads):
+        kcol = pair * 2 * QDIM
+        keys_ref[pair, cache_count:tree_end, :] = tree_pairs[:, kcol : kcol + QDIM]
+        keys_ref[pair, tree_end:, :] = none
+        values_ref[pair, cache_count:tree_end, :QDIM] = tree_pairs[:, kcol + QDIM : kcol + 2 * QDIM]
+        values_ref[pair, tree_end:, :QDIM] = none
+        first = query_start + pair * group_size * QDIM
+        query = ordered(first, group_size * QDIM).astype(BF16)
+        for g in range(group_size):
+            rows = slice(g * nodes, (g + 1) * nodes)
+            query_ref[pair, rows, :] = query[:, g * QDIM : (g + 1) * QDIM]
+
+    row_total = group_size * nodes
+
+    def score(pair, block):
+        keys = slice(block * LANES, (block + 1) * LANES)
+        score_ref[pair, :, keys] = last_dot(query_ref[pair], keys_ref[pair, keys, :])
+
+    def soften(pair, start):
+        rows = slice(start, start + 16)
+        node = start % nodes
+        cached = score_ref[pair, rows, :cache_count] + cache_bias
+        tree = score_ref[pair, rows, cache_count:] + tree_bias[node : node + 16]
+        part = jnp.concatenate([cached, tree], axis=1)
+        peak = jnp.max(part, axis=1, keepdims=True)
+        prob_ref[pair, rows, :] = jnp.exp2((part - peak) * scale).astype(BF16)
+
+    def attend(pair, start, count):
+        rows = slice(start, start + count)
+        result = jnp.dot(prob_ref[pair, rows, :], values_ref[pair], preferred_element_type=F32)
+        result = (result[:, :QDIM] / result[:, QDIM:]).astype(BF16)
+        for begin in range(0, count, nodes):
+            column = (pair * group_size + (start + begin) // nodes) * QDIM
+            attend_ref[:, column : column + QDIM] = result[begin : begin + nodes]
+
+    for load in loads[4:]:
+        load.wait()
+    key_blocks = keys_ref.shape[1] // LANES
+    scores = [(pair, block) for pair in range(pair_heads) for block in range(key_blocks)]
+    softs = [(pair, start) for pair in range(pair_heads) for start in range(0, row_total, 16)]
+    per_pair = row_total // 16
+    done_softs = 0
     for group in range(groups):
         proj = ordered(proj_start + group * 2 * STATE, 2 * STATE).astype(BF16)
         write_rows = proj[:, :STATE]
@@ -210,54 +265,29 @@
             weight = jnp.exp2(jnp.minimum(decay_i - decay_pairs[row], 0.0))
             weight_ref[:, lanes] = (weight * inner * step_pairs[row]).astype(BF16)
             base_ref[:, lanes] = jnp.exp2(decay_i) * carried
-            path_ref[:, lanes] = spread(columns, head_local + head)
             skip_out_ref[:, lanes] = spread(skip_columns, head)[0:1]
-            for index in range(head, head + wide):
-                kept_ref[index] = keep[index : index + 1, :] * state_ref[0, index].astype(F32)
-
-    group_size = query_width // QDIM // pair_heads
-    scale = QDIM ** (-0.5) * LOG2E
-    tree_pairs = ordered(kv_start, keyval_width).astype(BF16)
-    none = jnp.zeros((keys_ref.shape[1] - cache_count - nodes, QDIM), BF16)
-    tree_bias = ((1.0 - mask_t) * FAR).astype(BF16)
-    tree_bias = jnp.concatenate([tree_bias, jnp.zeros_like(tree_bias)], axis=1)
-    sub = lax.broadcasted_iota(jnp.int32, (nodes, LANES), 0)
-    lane = lax.broadcasted_iota(jnp.int32, (nodes, LANES), 1)
-    own_node = jnp.where(sub == lane, 1.0, 0.0).astype(BF16)
-    tree_end = cache_count + nodes
+            step_index = head // wide
+            if SCORE_EVERY and step_index % SCORE_EVERY == 0 and scores:
+                score(*scores.pop(0))
+            if SOFT_FROM <= step_index:
+                for _ in range(SOFT_EACH):
+                    if done_softs < per_pair:
+                        soften(*softs[done_softs])
+                        done_softs += 1
+    while scores:
+        score(*scores.pop(0))
+    while done_softs < per_pair:
+        soften(*softs[done_softs])
+        done_softs += 1
+    half_rows = row_total // ATTEND_PARTS
     for pair in range(pair_heads):
-        kcol = pair * 2 * QDIM
-        keys_ref[pair, cache_count:tree_end, :QDIM] = tree_pairs[:, kcol : kcol + QDIM]
-        keys_ref[pair, cache_count:tree_end, QDIM:] = tree_bias
-        keys_ref[pair, tree_end:, :QDIM] = none
-        keys_ref[pair, tree_end:, QDIM:] = jnp.full(none.shape, FAR, BF16)
-        values_ref[pair, cache_count:tree_end, :QDIM] = tree_pairs[:, kcol + QDIM : kcol + 2 * QDIM]
-        values_ref[pair, tree_end:, :QDIM] = none
-    for load in loads[5:]:
-        load.wait()
-    for pair in range(pair_heads):
-        first = pair * group_size * QDIM
-        query = ordered(query_start + first, group_size * QDIM).astype(BF16)
-        query = jnp.concatenate(
-            [
-                jnp.concatenate([query[:, g * QDIM : (g + 1) * QDIM], own_node], axis=1)
-                for g in range(group_size)
-            ],
-            axis=0,
-        )
-        score_ref[...] = last_dot(query, keys_ref[pair])
-        for start in range(0, group_size * nodes, 16):
-            rows = slice(start, start + 16)
-            score = score_ref[rows, :]
-            peak = jnp.max(score, axis=1, keepdims=True)
-            prob_ref[rows, :] = jnp.exp2((score - peak) * scale).astype(BF16)
-        for g in range(0, group_size, 2):
-            rows = slice(g * nodes, (g + 2) * nodes)
-            result = jnp.dot(prob_ref[rows, :], values_ref[pair], preferred_element_type=F32)
-            result = (result[:, :QDIM] / result[:, QDIM:]).astype(BF16)
-            for part in range(2):
-                column = first + (g + part) * QDIM
-                attend_ref[:, column : column + QDIM] = result[part * nodes : (part + 1) * nodes]
+        ahead = softs[done_softs : done_softs + per_pair]
+        done_softs += per_pair
+        share = -(-len(ahead) // ATTEND_PARTS)
+        for part in range(ATTEND_PARTS):
+            attend(pair, part * half_rows, half_rows)
+            for item in ahead[part * share : (part + 1) * share]:
+                soften(*item)
 
 
 def mix(first_offsets, second_offsets, late, *refs):
@@ -276,7 +306,12 @@
     chunk = 4 * LANES
 
     def ordered(start):
-        views = seconds if start < late else firsts
+        views = firsts
+        if seconds:
+            views = [
+                second if start < early_from else first
+                for first, second, early_from in zip(firsts, seconds, late)
+            ]
         return jnp.dot(order, joined(views, start, chunk), preferred_element_type=F32)
 
     ahead = ordered(0)
@@ -299,25 +334,28 @@
     store.wait()
 
 
-def advance(input_ref, path_ref, write_ref, kept_ref, out_ref):
-    head_local = kept_ref.shape[0]
+def advance(input_ref, columns_ref, write_ref, keep_ref, state_ref, out_ref):
+    head_local = state_ref.shape[1]
     groups = write_ref.shape[1] // STATE
     per_group = head_local // groups
-    width = per_group * HEAD_DIM
+    wide = LANES // HEAD_DIM
+    columns = columns_ref[...]
     for group in range(groups):
-        lanes = slice(group * width, (group + 1) * width)
-        weighted = (path_ref[:, lanes] * input_ref[:, lanes].astype(F32)).astype(BF16)
+        weighted = []
+        for pair in range(per_group // wide):
+            head = group * per_group + pair * wide
+            rows = input_ref[:, head * HEAD_DIM : head * HEAD_DIM + LANES].astype(F32)
+            weighted.append((spread(columns, head_local + head) * rows).astype(BF16))
         update = lax.dot_general(
-            weighted,
+            jnp.concatenate(weighted, axis=1),
             write_ref[:, group * STATE : (group + 1) * STATE],
             (((0,), (0,)), ((), ())),
             preferred_element_type=F32,
         )
         for index in range(per_group):
             head = group * per_group + index
-            out_ref[0, head] = (
-                kept_ref[head] + update[index * HEAD_DIM : (index + 1) * HEAD_DIM]
-            ).astype(BF16)
+            kept = keep_ref[head : head + 1, :] * state_ref[0, head].astype(F32)
+            out_ref[0, head] = (kept + update[index * HEAD_DIM : (index + 1) * HEAD_DIM]).astype(BF16)
 
 
 def finish(total_width, mixed_ref, mine_ref, other_ref, gain_ref, state_ref, *refs):
@@ -385,25 +423,30 @@
     head_shards = lax.axis_size("head")
     cap_rows = max(2, row_count // peers)
     slot_total = peers * cap_rows
-    direct = 4 <= peers <= 16 and peers & (peers - 1) == 0
+    direct = peers == len(EARLY_FROM)
+    assert row_count & (row_count - 1) == 0 and scan_width * 2 == LANES * HEAD_DIM
     head_local = scan_width // HEAD_DIM
     query_width = draft_query.shape[1]
     keyval_width = draft_keyval.shape[1]
     proj_width = draft_proj.shape[1]
     groups = proj_width // (2 * STATE)
     all_width = scan_width + query_width + keyval_width + proj_width + LANES
-    early = int(EARLY * scan_width) if direct else scan_width
-    late = scan_width - early
-    rest_width = all_width - late
+    late = 0
     if direct:
         odd = range(1, peers, 2)
         even = range(2, peers, 2)
+        unit = scan_width // 8
+        early_from = [EARLY_FROM[block] * unit for block in range(peers)]
         layout = [((0, 1, 0, all_width, 0),)]
-        layout += [((block, 1, late, all_width, 0),) for block in range(1, peers)]
-        layout += [((block, 1, 0, late, 0),) for block in even]
-        layout += [tuple((block, 1, 0, late, index * late) for index, block in enumerate(odd))]
-        widths = [all_width] + [rest_width] * (peers - 1)
-        widths += [late] * len(even) + [late * len(odd)]
+        layout += [((block, 1, early_from[block], all_width, 0),) for block in range(2, peers)]
+        layout += [((block, 1, 0, early_from[block], 0),) for block in even]
+        side, side_width = [(1, 1, 0, all_width, 0)], all_width
+        for block in odd[1:]:
+            side.append((block, 1, 0, early_from[block], side_width))
+            side_width += early_from[block]
+        layout += [tuple(side)]
+        widths = [all_width] + [all_width - early_from[block] for block in range(2, peers)]
+        widths += [max(early_from[block], LANES) for block in even] + [side_width]
         rows_of = cap_rows
     else:
         layout, widths = [((0, peers, 0, all_width, 0),)], [all_width]
@@ -423,37 +466,50 @@
         return lax.ppermute(block, "req", pairs)
 
     if direct:
-        own, rest, inputs = packed[0], packed[1:peers], packed[peers:]
+        own, rest, inputs = packed[0], packed[1 : peers - 1], packed[peers - 1 :]
         arrived = moved(inputs[-1], 1)
-        rest = [moved(block, step) for step, block in enumerate(rest, start=1)]
-        count = len(even)
-
-        def forward_all(*refs):
-            forward(refs[:count], refs[count], refs[count + 1 :])
-
-        pairs = call(
-            forward_all, "v" * (count + 1), (("v", (cap_rows, 2 * late), BF16),) * count
-        )(*inputs[:-1], arrived)
-        pairs = [moved(block, step) for step, block in zip(even, pairs)]
-        first_blocks, first_offsets = [own] + rest, [0] + [late] * (peers - 1)
+        rest = [moved(block, step) for step, block in enumerate(rest, start=2)]
+        later = [block for block in even if early_from[block] + early_from[block + 1]]
+        inputs = {block: part for block, part in zip(even, inputs)}
+        count = len(later)
+
+        def forward_all(accepted_ref, length_ref, *refs):
+            widths = [(early_from[block], early_from[block + 1]) for block in later]
+            skips = [sum(early_from[3:block:2]) for block in later]
+            forward(widths, refs[count], [all_width + skip for skip in skips], refs[:count], refs[count + 1 : -1])
+            lane = lax.broadcasted_iota(jnp.int32, refs[-1].shape, 1)
+            refs[-1][...] = jnp.where(lane == 0, accepted_ref[0], length_ref[0])
+
+        *pairs, scalars = call(
+            forward_all,
+            "ss" + "v" * (count + 1),
+            tuple(
+                ("v", (cap_rows, early_from[block] + early_from[block + 1]), BF16)
+                for block in later
+            )
+            + (("v", (8, LANES), jnp.int32),),
+        )(accepted, cache_length, *[inputs[block] for block in later], arrived)
+        pairs = {block: moved(part, block) for block, part in zip(later, pairs)}
+        first_blocks, first_offsets = [own, arrived] + rest, [0, 0] + early_from[2:]
         second_blocks, second_offsets = [own, arrived], [0, 0]
-        for block in pairs:
+        for step in even:
+            block = pairs.get(step, own)
             second_blocks += [block, block]
-            second_offsets += [0, -late]
+            second_offsets += [0, -early_from[step]]
+        late = early_from
     else:
         split = packed[0].reshape(peers, cap_rows, all_width)
         arrived = lax.all_to_all(split, "req", split_axis=0, concat_axis=0, tiled=True)
         first_blocks, first_offsets = [arrived.reshape(slot_total, all_width)], [0]
+        scalars = lax.pad(accepted, 0, [(0, LANES - 1, 0)])
+        scalars = scalars + lax.pad(cache_length, 0, [(1, LANES - 2, 0)])
+        scalars = jnp.broadcast_to(scalars, (8, LANES))
         second_blocks, second_offsets = [], []
 
-    scalars = lax.pad(accepted, 0, [(0, LANES - 1, 0)]) + lax.pad(
-        cache_length, 0, [(1, LANES - 2, 0)]
-    )
-    scalars = scalars.reshape(1, LANES)
     pair_heads = keyval_width // (2 * QDIM)
     score_rows = NODES * (query_width // QDIM // pair_heads)
     key_rows = cache_keyval.shape[1] + LANES
-    attended, weight, base, path, kept, write, order, skip_wide, gain = call(
+    attended, weight, base, columns, keep, write, order, skip_wide, gain, state = call(
         functools.partial(
             middle,
             first_offsets,
@@ -464,27 +520,28 @@
             ("v", (row_count, query_width), BF16),
             ("v", (NODES, head_local * NODES), BF16),
             ("v", (NODES, scan_width), F32),
-            ("v", (NODES, scan_width), F32),
-            ("v", (head_local, HEAD_DIM, STATE), F32),
+            ("v", (NODES, LANES), F32),
+            ("v", (head_local, LANES), F32),
             ("v", (NODES, groups * STATE), BF16),
             ("v", (NODES, slot_total), BF16),
             ("v", (1, scan_width), F32),
             ("v", (1, scan_width), F32),
+            ("v", scan_state.shape, BF16),
         ),
         scratch=[
             pltpu.VMEM(tree_mask.shape, jnp.int32),
             pltpu.VMEM((1, head_local), F32),
             pltpu.VMEM((1, head_local), F32),
             pltpu.VMEM((1, head_local), F32),
-            pltpu.VMEM(scan_state.shape, BF16),
+            pltpu.VMEM((pair_heads, key_rows, QDIM), BF16),
             pltpu.VMEM((pair_heads, key_rows, 2 * QDIM), BF16),
-            pltpu.VMEM((pair_heads, key_rows, 2 * QDIM), BF16),
-            pltpu.VMEM((score_rows, key_rows), F32),
-            pltpu.VMEM((score_rows, key_rows), BF16),
+            pltpu.VMEM((pair_heads, score_rows, QDIM), BF16),
+            pltpu.VMEM((pair_heads, score_rows, key_rows), F32),
+            pltpu.VMEM((pair_heads, score_rows, key_rows), BF16),
             pltpu.VMEM((2, head_local, LANES), F32),
             pltpu.SemaphoreType.DMA((6 + 2 * pair_heads,)),
         ],
-        mebibytes=24,
+        mebibytes=28,
     )(
         *first_blocks,
         scalars,
@@ -510,8 +567,8 @@
     )(*first_blocks, *second_blocks, order, weight, base, skip_wide, attended)
     swap = [(index, (index + 1) % head_shards) for index in range(head_shards)]
     other = lax.ppermute(square, "head", swap)
-    new_state = call(advance, "v" * 4, (("v", scan_state.shape, BF16),))(
-        inputs, path, write, kept
+    new_state = call(advance, "v" * 5, (("v", scan_state.shape, BF16),))(
+        inputs, columns, write, keep, state
     )[0]
     mixer_out, new_state = call(
         functools.partial(finish, head_shards * scan_width),

time: 44.3 us -> 50.5 us (1.14)
  the two profiles are of different devices: /device:TPU:13 before, /device:TPU:0 now
where the time goes in v2:
time: 50.5 us; the launch traced here: 50.3 us
  waiting for transfers between devices  21.2 us (42%)
  starting transfers between devices  16.9 us (33%)
  Pallas kernels  10.2 us (20%)
  between operations  2.01 us (4%)
    ppermute x10, waiting for transfers between devices, moved(): return lax.ppermute(block, 'req', pairs)  21.1 us
    ppermute x10, starting transfers between devices, moved(): return lax.ppermute(block, 'req', pairs)  16.8 us
    pallas_call x6, Pallas kernels, run(): pl.pallas_call(body, out_shape=tuple((SPACES[space](dims, kind) for space...  10.2 us
  transfers between devices with their start and end apart: 11, of which 4 were waited for; matrix products, arithmetic and copies ran while one was open for 0% of the time, Pallas kernels for 12%

profile of v2, /device:TPU:0, one launch (start us, length us, event | category | flops | bytes accessed | tf_op | source)
XLA Modules:
  0.0 50.3 jit_solution(3330005454205219518)
XLA Ops:
  0.6 2.0 %shard_map.166 = (bf16[8,7808]{1,0:T(8,128)(2,1)S(1)}, bf16[8,3712]{1,0:T(8,128)(2,1)S(1)}, bf16[8,3712]{1,0:T(8,128)(2,1)S(1)}, bf16[8,7808]{1,0:T(8,128)(2,1)S...) custom-call(s32[1,64]{1,0:T(1,128)} %bitcast.6, ...), custom_call_target="tpu_custom_call" | custom-call | tf_op jit(solution)/shard_map/pallas_call | solution.py:392
  2.7 3.0 %collective-permute-start = (bf16[8,20096]{1,0:T(8,128)(2,1)S(1)}, bf16[8,20096]{1,0:T(8,128)(2,1)S(1)}, u32[]{:S(2)}, u32[]{:S(2)}) collective-permute-start(bf16[8,20096]{1,0:T(8,128)(2,1)S(1)} %get-tuple-element.35), channel_id=1, source_target_pairs={{0,2},{2,0},{4,6},{6,4},{8,10},{10,8},{12,14},{14,12},{1,3},{3,1},... | collective-permute-start | bytes 964616 | tf_op jit(solution)/shard_map/ppermute | solution.py:466
  5.7 1.6 %collective-permute-start.1 = (bf16[8,3712]{1,0:T(8,128)(2,1)S(1)}, bf16[8,3712]{1,0:T(8,128)(2,1)S(1)}, u32[]{:S(2)}, u32[]{:S(2)}) collective-permute-start(bf16[8,3712]{1,0:T(8,128)(2,1)S(1)} %get-tuple-element.36), channel_id=1, source_target_pairs={{0,4},{2,6},{4,0},{6,2},{8,12},{10,14},{12,8},{14,10},{1,5},{3,7},... | collective-permute-start | bytes 178184 | tf_op jit(solution)/shard_map/ppermute | solution.py:466
  7.3 0.0 collective-permute-start.2
  8.6 6.0 %collective-permute-done.refs_3_.refs_1_.refs_9_ = bf16[8,20096]{1,0:T(8,128)(2,1)S(1)} collective-permute-done((bf16[8,20096]{1,0:T(8,128)(2,1)S(1)}, bf16[8,20096]{1,0:T(8,128)(2,1)S(1)}, u32[]{:S(2)}, u32[]{:S(2)}) %collective-permute-start) | collective-permute-done | bytes 321568 | tf_op jit(solution)/shard_map/ppermute | solution.py:466
  14.6 1.9 %collective-permute-start.7 = (bf16[8,8192]{1,0:T(8,128)(2,1)S(1)}, bf16[8,8192]{1,0:T(8,128)(2,1)S(1)}, u32[]{:S(2)}, u32[]{:S(2)}) collective-permute-start(bf16[8,8192]{1,0:T(8,128)(2,1)S(1)} %get-tuple-element.45), channel_id=1, source_target_pairs={{0,4},{2,6},{4,0},{6,2},{8,12},{10,14},{12,8},{14,10},{1,5},{3,7},... | collective-permute-start | bytes 393224 | tf_op jit(solution)/shard_map/ppermute | solution.py:466
  16.5 2.5 %collective-permute-start.9 = (bf16[8,8192]{1,0:T(8,128)(2,1)S(1)}, bf16[8,8192]{1,0:T(8,128)(2,1)S(1)}, u32[]{:S(2)}, u32[]{:S(2)}) collective-permute-start(bf16[8,8192]{1,0:T(8,128)(2,1)S(1)} %get-tuple-element.47), channel_id=1, source_target_pairs={{0,12},{2,14},{4,8},{6,10},{8,4},{10,6},{12,0},{14,2},{1,13},{3,15... | collective-permute-start | bytes 393224 | tf_op jit(solution)/shard_map/ppermute | solution.py:466
  19.0 0.1 collective-permute-start.3
  19.1 0.0 collective-permute-done.1.refs_2_
  19.1 3.7 %collective-permute-start.4 = (bf16[8,3712]{1,0:T(8,128)(2,1)S(1)}, bf16[8,3712]{1,0:T(8,128)(2,1)S(1)}, u32[]{:S(2)}, u32[]{:S(2)}) collective-permute-start(bf16[8,3712]{1,0:T(8,128)(2,1)S(1)} %get-tuple-element.39), channel_id=1, source_target_pairs={{0,10},{2,8},{4,14},{6,12},{8,2},{10,0},{12,6},{14,4},{1,11},{3,9}... | collective-permute-start | bytes 178184 | tf_op jit(solution)/shard_map/ppermute | solution.py:466
  22.8 0.0 collective-permute-done.2.refs_3_
  22.8 1.4 %collective-permute-start.5 = (bf16[8,3712]{1,0:T(8,128)(2,1)S(1)}, bf16[8,3712]{1,0:T(8,128)(2,1)S(1)}, u32[]{:S(2)}, u32[]{:S(2)}) collective-permute-start(bf16[8,3712]{1,0:T(8,128)(2,1)S(1)} %get-tuple-element.40), channel_id=1, source_target_pairs={{0,12},{2,14},{4,8},{6,10},{8,4},{10,6},{12,0},{14,2},{1,13},{3,15... | collective-permute-start | bytes 178184 | tf_op jit(solution)/shard_map/ppermute | solution.py:466
  24.2 10.8 %collective-permute-done.4.refs_5_ = bf16[8,3712]{1,0:T(8,128)(2,1)S(1)} collective-permute-done((bf16[8,3712]{1,0:T(8,128)(2,1)S(1)}, bf16[8,3712]{1,0:T(8,128)(2,1)S(1)}, u32[]{:S(2)}, u32[]{:S(2)}) %collective-permute-start.4) | collective-permute-done | bytes 59424 | tf_op jit(solution)/shard_map/ppermute | solution.py:466
  35.0 0.0 collective-permute-start.8
  35.0 0.0 collective-permute-done.5.refs_6_
  35.0 2.6 %collective-permute-start.6 = (bf16[8,3712]{1,0:T(8,128)(2,1)S(1)}, bf16[8,3712]{1,0:T(8,128)(2,1)S(1)}, u32[]{:S(2)}, u32[]{:S(2)}) collective-permute-start(bf16[8,3712]{1,0:T(8,128)(2,1)S(1)} %get-tuple-element.41), channel_id=1, source_target_pairs={{0,14},{2,12},{4,10},{6,8},{8,6},{10,4},{12,2},{14,0},{1,15},{3,13... | collective-permute-start | bytes 178184 | tf_op jit(solution)/shard_map/ppermute | solution.py:466
  37.6 4.3 %collective-permute-done.6.refs_7_ = bf16[8,3712]{1,0:T(8,128)(2,1)S(1)} collective-permute-done((bf16[8,3712]{1,0:T(8,128)(2,1)S(1)}, bf16[8,3712]{1,0:T(8,128)(2,1)S(1)}, u32[]{:S(2)}, u32[]{:S(2)}) %collective-permute-start.6) | collective-permute-done | bytes 59424 | tf_op jit(solution)/shard_map/ppermute | solution.py:466
  41.9 0.0 collective-permute-done.3.refs_4_
  41.9 4.9 %shard_map.168 = (bf16[64,2048]{1,0:T(8,128)(2,1)S(1)}, bf16[64,4096]{1,0:T(8,128)(2,1)S(1)}, f32[64,4096]{1,0:T(8,128)S(1)}, f32[64,128]{1,0:T(8,128)S(1)}, f32...) custom-call(bf16[8,7808]{1,0:T(8,128)(2,1)S(1)} %get-tuple-element.3, ...), custom_call_target="tpu_custom_call" | custom-call | tf_op jit(solution)/shard_map/pallas_call | solution.py:392
  46.8 0.0 collective-permute-done.8.refs_12_.refs_13_
  46.8 0.0 collective-permute-done.7.refs_10_.refs_11_
  46.8 0.0 collective-permute-done.9.refs_14_.refs_15_
  46.8 1.1 %shard_map.169 = (f32[64,4096]{1,0:T(8,128)S(1)}, f32[64,128]{1,0:T(8,128)S(1)}, bf16[64,4096]{1,0:T(8,128)(2,1)S(1)}, bf16[64,2048]{1,0:T(8,128)(2,1)}) custom-call(bf16[8,7808]{1,0:T(8,128)(2,1)S(1)} %get-tuple-element.34.refs_0_.refs_8_, bf16[8,20096]{1,0:T(8,128)(2,1)S(1)} %collective-permute-done.refs_3_.refs_1_.refs_9_, ...), custom_call_target="tpu_custom_call" | custom-call | tf_op jit(solution)/shard_map/pallas_call | solution.py:392
  47.9 0.1 collective-permute-start.10
  47.9 1.0 %shard_map.170.state_ref = bf16[1,64,64,128]{3,2,1,0:T(8,128)(2,1)S(1)} custom-call(bf16[64,4096]{1,0:T(8,128)(2,1)S(1)} %get-tuple-element.57.input_ref, f32[64,128]{1,0:T(8,128)S(1)} %get-tuple-element.58.columns_ref, bf16[64,512]{1,0:T(8,128)(2,1)S(1)} %get-tuple-element.59.write_ref, f32[64,128]{1,0:T(8,128)S(1)} %get-tuple-element.60.keep_ref, ...), custom_call_target="tpu_custom_call" | custom-call | tf_op jit(solution)/shard_map/pallas_call | solution.py:392
  49.0 0.2 collective-permute-done.10.other_ref
  49.1 1.2 %shard_map.171 = (bf16[64,4096]{1,0:T(8,128)(2,1)}, bf16[1,64,64,128]{3,2,1,0:T(8,128)(2,1)}) custom-call(f32[64,4096]{1,0:T(8,128)S(1)} %get-tuple-element.54.mixed_ref, f32[64,128]{1,0:T(8,128)S(1)} %get-tuple-element.55.mine_ref, f32[64,128]{1,0:T(8,128)S(1)} %collective-permute-done.10.other_ref, f32[1,4096]{1,0:T(1,128)S(1)} %get-tuple-element.56.gain_ref, ...), custom_call_target="tpu_custom_call" | custom-call | tf_op jit(solution)/shard_map/pallas_call | solution.py:392
  (1 shorter events, 0.0 us)
Async XLA Ops:
  2.7 11.9 %collective-permute-start = (bf16[8,20096]{1,0:T(8,128)(2,1)S(1)}, bf16[8,20096]{1,0:T(8,128)(2,1)S(1)}, u32[]{:S(2)}, u32[]{:S(2)}) collective-permute-start(bf16[8,20096]{1,0:T(8,128)(2,1)S(1)} %get-tuple-element.35), channel_id=1, source_target_pairs={{0,2},{2,0},{4,6},{6,4},{8,10},{10,8},{12,14},{14,12},{1,3},{3,1},... | collective-permute-start | bytes 964616 | tf_op jit(solution)/shard_map/ppermute | solution.py:466
  5.7 13.4 %collective-permute-start.1 = (bf16[8,3712]{1,0:T(8,128)(2,1)S(1)}, bf16[8,3712]{1,0:T(8,128)(2,1)S(1)}, u32[]{:S(2)}, u32[]{:S(2)}) collective-permute-start(bf16[8,3712]{1,0:T(8,128)(2,1)S(1)} %get-tuple-element.36), channel_id=1, source_target_pairs={{0,4},{2,6},{4,0},{6,2},{8,12},{10,14},{12,8},{14,10},{1,5},{3,7},... | collective-permute-start | bytes 178184 | tf_op jit(solution)/shard_map/ppermute | solution.py:466
  7.3 15.5 %collective-permute-start.2 = (bf16[8,3712]{1,0:T(8,128)(2,1)S(1)}, bf16[8,3712]{1,0:T(8,128)(2,1)S(1)}, u32[]{:S(2)}, u32[]{:S(2)}) collective-permute-start(bf16[8,3712]{1,0:T(8,128)(2,1)S(1)} %get-tuple-element.37), channel_id=1, source_target_pairs={{0,6},{2,4},{4,2},{6,0},{8,14},{10,12},{12,10},{14,8},{1,7},{3,5},... | collective-permute-start | bytes 178184 | tf_op jit(solution)/shard_map/ppermute | solution.py:466
  14.6 32.2 %collective-permute-start.7 = (bf16[8,8192]{1,0:T(8,128)(2,1)S(1)}, bf16[8,8192]{1,0:T(8,128)(2,1)S(1)}, u32[]{:S(2)}, u32[]{:S(2)}) collective-permute-start(bf16[8,8192]{1,0:T(8,128)(2,1)S(1)} %get-tuple-element.45), channel_id=1, source_target_pairs={{0,4},{2,6},{4,0},{6,2},{8,12},{10,14},{12,8},{14,10},{1,5},{3,7},... | collective-permute-start | bytes 393224 | tf_op jit(solution)/shard_map/ppermute | solution.py:466
  16.5 30.3 %collective-permute-start.9 = (bf16[8,8192]{1,0:T(8,128)(2,1)S(1)}, bf16[8,8192]{1,0:T(8,128)(2,1)S(1)}, u32[]{:S(2)}, u32[]{:S(2)}) collective-permute-start(bf16[8,8192]{1,0:T(8,128)(2,1)S(1)} %get-tuple-element.47), channel_id=1, source_target_pairs={{0,12},{2,14},{4,8},{6,10},{8,4},{10,6},{12,0},{14,2},{1,13},{3,15... | collective-permute-start | bytes 393224 | tf_op jit(solution)/shard_map/ppermute | solution.py:466
  19.0 22.9 %collective-permute-start.3 = (bf16[8,7808]{1,0:T(8,128)(2,1)S(1)}, bf16[8,7808]{1,0:T(8,128)(2,1)S(1)}, u32[]{:S(2)}, u32[]{:S(2)}) collective-permute-start(bf16[8,7808]{1,0:T(8,128)(2,1)S(1)} %get-tuple-element.38), channel_id=1, source_target_pairs={{0,8},{2,10},{4,12},{6,14},{8,0},{10,2},{12,4},{14,6},{1,9},{3,11}... | collective-permute-start | bytes 374792 | tf_op jit(solution)/shard_map/ppermute | solution.py:466
  19.1 15.9 %collective-permute-start.4 = (bf16[8,3712]{1,0:T(8,128)(2,1)S(1)}, bf16[8,3712]{1,0:T(8,128)(2,1)S(1)}, u32[]{:S(2)}, u32[]{:S(2)}) collective-permute-start(bf16[8,3712]{1,0:T(8,128)(2,1)S(1)} %get-tuple-element.39), channel_id=1, source_target_pairs={{0,10},{2,8},{4,14},{6,12},{8,2},{10,0},{12,6},{14,4},{1,11},{3,9}... | collective-permute-start | bytes 178184 | tf_op jit(solution)/shard_map/ppermute | solution.py:466
  22.8 12.2 %collective-permute-start.5 = (bf16[8,3712]{1,0:T(8,128)(2,1)S(1)}, bf16[8,3712]{1,0:T(8,128)(2,1)S(1)}, u32[]{:S(2)}, u32[]{:S(2)}) collective-permute-start(bf16[8,3712]{1,0:T(8,128)(2,1)S(1)} %get-tuple-element.40), channel_id=1, source_target_pairs={{0,12},{2,14},{4,8},{6,10},{8,4},{10,6},{12,0},{14,2},{1,13},{3,15... | collective-permute-start | bytes 178184 | tf_op jit(solution)/shard_map/ppermute | solution.py:466
  35.0 11.8 %collective-permute-start.8 = (bf16[8,4096]{1,0:T(8,128)(2,1)S(1)}, bf16[8,4096]{1,0:T(8,128)(2,1)S(1)}, u32[]{:S(2)}, u32[]{:S(2)}) collective-permute-start(bf16[8,4096]{1,0:T(8,128)(2,1)S(1)} %get-tuple-element.46), channel_id=1, source_target_pairs={{0,8},{2,10},{4,12},{6,14},{8,0},{10,2},{12,4},{14,6},{1,9},{3,11}... | collective-permute-start | bytes 196616 | tf_op jit(solution)/shard_map/ppermute | solution.py:466
  35.0 6.9 %collective-permute-start.6 = (bf16[8,3712]{1,0:T(8,128)(2,1)S(1)}, bf16[8,3712]{1,0:T(8,128)(2,1)S(1)}, u32[]{:S(2)}, u32[]{:S(2)}) collective-permute-start(bf16[8,3712]{1,0:T(8,128)(2,1)S(1)} %get-tuple-element.41), channel_id=1, source_target_pairs={{0,14},{2,12},{4,10},{6,8},{8,6},{10,4},{12,2},{14,0},{1,15},{3,13... | collective-permute-start | bytes 178184 | tf_op jit(solution)/shard_map/ppermute | solution.py:466
  47.9 1.3 %collective-permute-start.10 = (f32[64,128]{1,0:T(8,128)S(1)}, f32[64,128]{1,0:T(8,128)S(1)}, u32[]{:S(2)}, u32[]{:S(2)}) collective-permute-start(f32[64,128]{1,0:T(8,128)S(1)} %get-tuple-element.55.mine_ref), channel_id=1, source_target_pairs={{0,1},{1,0},{2,3},{3,2},{4,5},{5,4},{6,7},{7,6},{8,9},{9,8},{10,11... | collective-permute-start | bytes 98312 | tf_op jit(solution)/shard_map/ppermute | solution.py:569

commit v3 on v2

--- a/solution.py
+++ b/solution.py
@@ -15,11 +15,11 @@
 LANES = 128
 LOG2E = 1.4426950408889634
 FAR = -1e30
-EARLY_FROM = (8, 8, 8, 8, 0, 8, 8, 8)
+EARLY_FROM = (8, 8, 8, 7, 0, 8, 8, 8)
 SCORE_EVERY = 1
 SOFT_FROM = 12
 SOFT_EACH = 2
-ATTEND_PARTS = 4
+ATTEND_PARTS = 2
 F32 = jnp.float32
 BF16 = jnp.bfloat16
 
@@ -118,7 +118,7 @@
     attend_ref, weight_ref, base_ref, columns_ref, keep_ref = refs[8:13]
     write_ref, order_ref, skip_out_ref, gain_ref = refs[13:17]
     state_ref, mask_ref, decay_ref, bias_ref, skip_ref, keys_ref, values_ref = refs[17:24]
-    query_ref, score_ref, prob_ref, rows_ref, sems = refs[24:]
+    query_ref, score_ref, prob_ref, total_ref, rows_ref, sems = refs[24:]
     pair_heads = keyval_width // (2 * QDIM)
     cache_count = cache_hbm.shape[1]
     sources = [mask_hbm, decay_hbm, bias_hbm, skip_hbm]
@@ -152,8 +152,6 @@
     length = scalar_ref[0:1, 1:2]
     position = lax.broadcasted_iota(jnp.int32, (1, cache_count), 1)
     cache_bias = jnp.where(position < length, 0.0, FAR)
-    for pair in range(pair_heads):
-        values_ref[pair, :, QDIM:] = jnp.ones((values_ref.shape[1], LANES), BF16)
 
     for load in loads[:4]:
         load.wait()
@@ -210,8 +208,8 @@
         kcol = pair * 2 * QDIM
         keys_ref[pair, cache_count:tree_end, :] = tree_pairs[:, kcol : kcol + QDIM]
         keys_ref[pair, tree_end:, :] = none
-        values_ref[pair, cache_count:tree_end, :QDIM] = tree_pairs[:, kcol + QDIM : kcol + 2 * QDIM]
-        values_ref[pair, tree_end:, :QDIM] = none
+        values_ref[pair, cache_count:tree_end, :] = tree_pairs[:, kcol + QDIM : kcol + 2 * QDIM]
+        values_ref[pair, tree_end:, :] = none
         first = query_start + pair * group_size * QDIM
         query = ordered(first, group_size * QDIM).astype(BF16)
         for g in range(group_size):
@@ -231,12 +229,15 @@
         tree = score_ref[pair, rows, cache_count:] + tree_bias[node : node + 16]
         part = jnp.concatenate([cached, tree], axis=1)
         peak = jnp.max(part, axis=1, keepdims=True)
-        prob_ref[pair, rows, :] = jnp.exp2((part - peak) * scale).astype(BF16)
+        prob = jnp.exp2((part - peak) * scale)
+        total = jnp.sum(prob, axis=1, keepdims=True)
+        total_ref[pair, rows, :] = jnp.broadcast_to(total, (16, QDIM))
+        prob_ref[pair, rows, :] = prob.astype(BF16)
 
     def attend(pair, start, count):
         rows = slice(start, start + count)
         result = jnp.dot(prob_ref[pair, rows, :], values_ref[pair], preferred_element_type=F32)
-        result = (result[:, :QDIM] / result[:, QDIM:]).astype(BF16)
+        result = (result / total_ref[pair, rows, :]).astype(BF16)
         for begin in range(0, count, nodes):
             column = (pair * group_size + (start + begin) // nodes) * QDIM
             attend_ref[:, column : column + QDIM] = result[begin : begin + nodes]
@@ -534,10 +535,11 @@
             pltpu.VMEM((1, head_local), F32),
             pltpu.VMEM((1, head_local), F32),
             pltpu.VMEM((pair_heads, key_rows, QDIM), BF16),
-            pltpu.VMEM((pair_heads, key_rows, 2 * QDIM), BF16),
+            pltpu.VMEM((pair_heads, key_rows, QDIM), BF16),
             pltpu.VMEM((pair_heads, score_rows, QDIM), BF16),
             pltpu.VMEM((pair_heads, score_rows, key_rows), F32),
             pltpu.VMEM((pair_heads, score_rows, key_rows), BF16),
+            pltpu.VMEM((pair_heads, score_rows, QDIM), F32),
             pltpu.VMEM((2, head_local, LANES), F32),
             pltpu.SemaphoreType.DMA((6 + 2 * pair_heads,)),
         ],

time: 50.5 us -> 44.3 us (0.88)
  waiting for transfers between devices: 21.2 us -> 5.11 us
  starting transfers between devices: 16.9 us -> 27 us
    ppermute x10, waiting for transfers between devices: 21.1 us -> 4.93 us  [moved(): return lax.ppermute(block, 'req', pairs)]
    ppermute x10, starting transfers between devices: 16.8 us -> 26.9 us  [moved(): return lax.ppermute(block, 'req', pairs)]
  transfers between devices with their start and end apart: 11 -> 11, of which waited for: 4 -> 3; matrix products, arithmetic and copies ran while one was open for 0% -> 0% of each run, Pallas kernels for 12% -> 13%
where the time goes in v3:
time: 44.3 us; the launch traced here: 44.1 us
  starting transfers between devices  27 us (61%)
  Pallas kernels  9.98 us (23%)
  waiting for transfers between devices  5.11 us (12%)
  between operations  2.01 us (5%)
    ppermute x10, starting transfers between devices, moved(): return lax.ppermute(block, 'req', pairs)  26.9 us
    pallas_call x6, Pallas kernels, run(): pl.pallas_call(body, out_shape=tuple((SPACES[space](dims, kind) for space...  9.98 us
    ppermute x10, waiting for transfers between devices, moved(): return lax.ppermute(block, 'req', pairs)  4.93 us
  transfers between devices with their start and end apart: 11, of which 3 were waited for; matrix products, arithmetic and copies ran while one was open for 0% of the time, Pallas kernels for 13%

profile of v3, /device:TPU:0, one launch (start us, length us, event | category | flops | bytes accessed | tf_op | source)
XLA Modules:
  0.0 44.1 jit_solution(8285195107202775445)
XLA Ops:
  0.6 2.0 %shard_map.166 = (bf16[8,7808]{1,0:T(8,128)(2,1)S(1)}, bf16[8,3712]{1,0:T(8,128)(2,1)S(1)}, bf16[8,4224]{1,0:T(8,128)(2,1)S(1)}, bf16[8,7808]{1,0:T(8,128)(2,1)S...) custom-call(s32[1,64]{1,0:T(1,128)} %bitcast.6, ...), custom_call_target="tpu_custom_call" | custom-call | tf_op jit(solution)/shard_map/pallas_call | solution.py:393
  2.7 3.0 %collective-permute-start = (bf16[8,19584]{1,0:T(8,128)(2,1)S(1)}, bf16[8,19584]{1,0:T(8,128)(2,1)S(1)}, u32[]{:S(2)}, u32[]{:S(2)}) collective-permute-start(bf16[8,19584]{1,0:T(8,128)(2,1)S(1)} %get-tuple-element.35), channel_id=1, source_target_pairs={{0,2},{2,0},{4,6},{6,4},{8,10},{10,8},{12,14},{14,12},{1,3},{3,1},... | collective-permute-start | bytes 940040 | tf_op jit(solution)/shard_map/ppermute | solution.py:467
  5.7 1.6 %collective-permute-start.1 = (bf16[8,3712]{1,0:T(8,128)(2,1)S(1)}, bf16[8,3712]{1,0:T(8,128)(2,1)S(1)}, u32[]{:S(2)}, u32[]{:S(2)}) collective-permute-start(bf16[8,3712]{1,0:T(8,128)(2,1)S(1)} %get-tuple-element.36), channel_id=1, source_target_pairs={{0,4},{2,6},{4,0},{6,2},{8,12},{10,14},{12,8},{14,10},{1,5},{3,7},... | collective-permute-start | bytes 178184 | tf_op jit(solution)/shard_map/ppermute | solution.py:467
  7.3 2.6 %collective-permute-start.4 = (bf16[8,3712]{1,0:T(8,128)(2,1)S(1)}, bf16[8,3712]{1,0:T(8,128)(2,1)S(1)}, u32[]{:S(2)}, u32[]{:S(2)}) collective-permute-start(bf16[8,3712]{1,0:T(8,128)(2,1)S(1)} %get-tuple-element.39), channel_id=1, source_target_pairs={{0,10},{2,8},{4,14},{6,12},{8,2},{10,0},{12,6},{14,4},{1,11},{3,9}... | collective-permute-start | bytes 178184 | tf_op jit(solution)/shard_map/ppermute | solution.py:467
  11.1 3.2 %collective-permute-done.refs_3_.refs_1_.refs_9_ = bf16[8,19584]{1,0:T(8,128)(2,1)S(1)} collective-permute-done((bf16[8,19584]{1,0:T(8,128)(2,1)S(1)}, bf16[8,19584]{1,0:T(8,128)(2,1)S(1)}, u32[]{:S(2)}, u32[]{:S(2)}) %collective-permute-start) | collective-permute-done | bytes 313376 | tf_op jit(solution)/shard_map/ppermute | solution.py:467
  14.4 3.9 %collective-permute-start.9 = (bf16[8,8192]{1,0:T(8,128)(2,1)S(1)}, bf16[8,8192]{1,0:T(8,128)(2,1)S(1)}, u32[]{:S(2)}, u32[]{:S(2)}) collective-permute-start(bf16[8,8192]{1,0:T(8,128)(2,1)S(1)} %get-tuple-element.47), channel_id=1, source_target_pairs={{0,12},{2,14},{4,8},{6,10},{8,4},{10,6},{12,0},{14,2},{1,13},{3,15... | collective-permute-start | bytes 393224 | tf_op jit(solution)/shard_map/ppermute | solution.py:467
  18.3 0.1 collective-permute-start.5
  18.4 0.9 %collective-permute-start.3 = (bf16[8,7808]{1,0:T(8,128)(2,1)S(1)}, bf16[8,7808]{1,0:T(8,128)(2,1)S(1)}, u32[]{:S(2)}, u32[]{:S(2)}) collective-permute-start(bf16[8,7808]{1,0:T(8,128)(2,1)S(1)} %get-tuple-element.38), channel_id=1, source_target_pairs={{0,8},{2,10},{4,12},{6,14},{8,0},{10,2},{12,4},{14,6},{1,9},{3,11}... | collective-permute-start | bytes 374792 | tf_op jit(solution)/shard_map/ppermute | solution.py:467
  19.3 0.0 collective-permute-done.1.refs_2_
  19.3 3.7 %collective-permute-start.6 = (bf16[8,3712]{1,0:T(8,128)(2,1)S(1)}, bf16[8,3712]{1,0:T(8,128)(2,1)S(1)}, u32[]{:S(2)}, u32[]{:S(2)}) collective-permute-start(bf16[8,3712]{1,0:T(8,128)(2,1)S(1)} %get-tuple-element.41), channel_id=1, source_target_pairs={{0,14},{2,12},{4,10},{6,8},{8,6},{10,4},{12,2},{14,0},{1,15},{3,13... | collective-permute-start | bytes 178184 | tf_op jit(solution)/shard_map/ppermute | solution.py:467
  23.1 0.0 collective-permute-done.4.refs_5_
  23.1 0.0 collective-permute-start.7
  23.1 1.7 %collective-permute-done.5.refs_6_ = bf16[8,3712]{1,0:T(8,128)(2,1)S(1)} collective-permute-done((bf16[8,3712]{1,0:T(8,128)(2,1)S(1)}, bf16[8,3712]{1,0:T(8,128)(2,1)S(1)}, u32[]{:S(2)}, u32[]{:S(2)}) %collective-permute-start.5) | collective-permute-done | bytes 59424 | tf_op jit(solution)/shard_map/ppermute | solution.py:467
  24.8 7.2 %collective-permute-start.2 = (bf16[8,4224]{1,0:T(8,128)(2,1)S(1)}, bf16[8,4224]{1,0:T(8,128)(2,1)S(1)}, u32[]{:S(2)}, u32[]{:S(2)}) collective-permute-start(bf16[8,4224]{1,0:T(8,128)(2,1)S(1)} %get-tuple-element.37), channel_id=1, source_target_pairs={{0,6},{2,4},{4,2},{6,0},{8,14},{10,12},{12,10},{14,8},{1,7},{3,5},... | collective-permute-start | bytes 202760 | tf_op jit(solution)/shard_map/ppermute | solution.py:467
  32.0 0.0 collective-permute-done.6.refs_7_
  32.0 3.9 %collective-permute-start.8 = (bf16[8,4096]{1,0:T(8,128)(2,1)S(1)}, bf16[8,4096]{1,0:T(8,128)(2,1)S(1)}, u32[]{:S(2)}, u32[]{:S(2)}) collective-permute-start(bf16[8,4096]{1,0:T(8,128)(2,1)S(1)} %get-tuple-element.46), channel_id=1, source_target_pairs={{0,8},{2,10},{4,12},{6,14},{8,0},{10,2},{12,4},{14,6},{1,9},{3,11}... | collective-permute-start | bytes 196616 | tf_op jit(solution)/shard_map/ppermute | solution.py:467
  35.9 0.0 collective-permute-done.2.refs_3_
  35.9 0.0 collective-permute-done.3.refs_4_
  35.9 4.7 %shard_map.168 = (bf16[64,2048]{1,0:T(8,128)(2,1)S(1)}, bf16[64,4096]{1,0:T(8,128)(2,1)S(1)}, f32[64,4096]{1,0:T(8,128)S(1)}, f32[64,128]{1,0:T(8,128)S(1)}, f32...) custom-call(bf16[8,7808]{1,0:T(8,128)(2,1)S(1)} %get-tuple-element.3, ...), custom_call_target="tpu_custom_call" | custom-call | tf_op jit(solution)/shard_map/pallas_call | solution.py:393
  40.6 0.0 collective-permute-done.8.refs_12_.refs_13_
  40.6 0.0 collective-permute-done.7.refs_10_.refs_11_
  40.6 0.0 collective-permute-done.9.refs_14_.refs_15_
  40.6 1.1 %shard_map.169 = (f32[64,4096]{1,0:T(8,128)S(1)}, f32[64,128]{1,0:T(8,128)S(1)}, bf16[64,4096]{1,0:T(8,128)(2,1)S(1)}, bf16[64,2048]{1,0:T(8,128)(2,1)}) custom-call(bf16[8,7808]{1,0:T(8,128)(2,1)S(1)} %get-tuple-element.34.refs_0_.refs_8_, bf16[8,19584]{1,0:T(8,128)(2,1)S(1)} %collective-permute-done.refs_3_.refs_1_.refs_9_, ...), custom_call_target="tpu_custom_call" | custom-call | tf_op jit(solution)/shard_map/pallas_call | solution.py:393
  41.7 0.1 collective-permute-start.10
  41.7 1.0 %shard_map.170.state_ref = bf16[1,64,64,128]{3,2,1,0:T(8,128)(2,1)S(1)} custom-call(bf16[64,4096]{1,0:T(8,128)(2,1)S(1)} %get-tuple-element.57.input_ref, f32[64,128]{1,0:T(8,128)S(1)} %get-tuple-element.58.columns_ref, bf16[64,512]{1,0:T(8,128)(2,1)S(1)} %get-tuple-element.59.write_ref, f32[64,128]{1,0:T(8,128)S(1)} %get-tuple-element.60.keep_ref, ...), custom_call_target="tpu_custom_call" | custom-call | tf_op jit(solution)/shard_map/pallas_call | solution.py:393
  42.8 0.2 collective-permute-done.10.other_ref
  42.9 1.2 %shard_map.171 = (bf16[64,4096]{1,0:T(8,128)(2,1)}, bf16[1,64,64,128]{3,2,1,0:T(8,128)(2,1)}) custom-call(f32[64,4096]{1,0:T(8,128)S(1)} %get-tuple-element.54.mixed_ref, f32[64,128]{1,0:T(8,128)S(1)} %get-tuple-element.55.mine_ref, f32[64,128]{1,0:T(8,128)S(1)} %collective-permute-done.10.other_ref, f32[1,4096]{1,0:T(1,128)S(1)} %get-tuple-element.56.gain_ref, ...), custom_call_target="tpu_custom_call" | custom-call | tf_op jit(solution)/shard_map/pallas_call | solution.py:393
  (1 shorter events, 0.0 us)
Async XLA Ops:
  2.7 11.7 %collective-permute-start = (bf16[8,19584]{1,0:T(8,128)(2,1)S(1)}, bf16[8,19584]{1,0:T(8,128)(2,1)S(1)}, u32[]{:S(2)}, u32[]{:S(2)}) collective-permute-start(bf16[8,19584]{1,0:T(8,128)(2,1)S(1)} %get-tuple-element.35), channel_id=1, source_target_pairs={{0,2},{2,0},{4,6},{6,4},{8,10},{10,8},{12,14},{14,12},{1,3},{3,1},... | collective-permute-start | bytes 940040 | tf_op jit(solution)/shard_map/ppermute | solution.py:467
  5.7 13.6 %collective-permute-start.1 = (bf16[8,3712]{1,0:T(8,128)(2,1)S(1)}, bf16[8,3712]{1,0:T(8,128)(2,1)S(1)}, u32[]{:S(2)}, u32[]{:S(2)}) collective-permute-start(bf16[8,3712]{1,0:T(8,128)(2,1)S(1)} %get-tuple-element.36), channel_id=1, source_target_pairs={{0,4},{2,6},{4,0},{6,2},{8,12},{10,14},{12,8},{14,10},{1,5},{3,7},... | collective-permute-start | bytes 178184 | tf_op jit(solution)/shard_map/ppermute | solution.py:467
  7.3 15.8 %collective-permute-start.4 = (bf16[8,3712]{1,0:T(8,128)(2,1)S(1)}, bf16[8,3712]{1,0:T(8,128)(2,1)S(1)}, u32[]{:S(2)}, u32[]{:S(2)}) collective-permute-start(bf16[8,3712]{1,0:T(8,128)(2,1)S(1)} %get-tuple-element.39), channel_id=1, source_target_pairs={{0,10},{2,8},{4,14},{6,12},{8,2},{10,0},{12,6},{14,4},{1,11},{3,9}... | collective-permute-start | bytes 178184 | tf_op jit(solution)/shard_map/ppermute | solution.py:467
  14.4 26.2 %collective-permute-start.9 = (bf16[8,8192]{1,0:T(8,128)(2,1)S(1)}, bf16[8,8192]{1,0:T(8,128)(2,1)S(1)}, u32[]{:S(2)}, u32[]{:S(2)}) collective-permute-start(bf16[8,8192]{1,0:T(8,128)(2,1)S(1)} %get-tuple-element.47), channel_id=1, source_target_pairs={{0,12},{2,14},{4,8},{6,10},{8,4},{10,6},{12,0},{14,2},{1,13},{3,15... | collective-permute-start | bytes 393224 | tf_op jit(solution)/shard_map/ppermute | solution.py:467
  18.3 6.4 %collective-permute-start.5 = (bf16[8,3712]{1,0:T(8,128)(2,1)S(1)}, bf16[8,3712]{1,0:T(8,128)(2,1)S(1)}, u32[]{:S(2)}, u32[]{:S(2)}) collective-permute-start(bf16[8,3712]{1,0:T(8,128)(2,1)S(1)} %get-tuple-element.40), channel_id=1, source_target_pairs={{0,12},{2,14},{4,8},{6,10},{8,4},{10,6},{12,0},{14,2},{1,13},{3,15... | collective-permute-start | bytes 178184 | tf_op jit(solution)/shard_map/ppermute | solution.py:467
  18.4 17.5 %collective-permute-start.3 = (bf16[8,7808]{1,0:T(8,128)(2,1)S(1)}, bf16[8,7808]{1,0:T(8,128)(2,1)S(1)}, u32[]{:S(2)}, u32[]{:S(2)}) collective-permute-start(bf16[8,7808]{1,0:T(8,128)(2,1)S(1)} %get-tuple-element.38), channel_id=1, source_target_pairs={{0,8},{2,10},{4,12},{6,14},{8,0},{10,2},{12,4},{14,6},{1,9},{3,11}... | collective-permute-start | bytes 374792 | tf_op jit(solution)/shard_map/ppermute | solution.py:467
  19.3 12.6 %collective-permute-start.6 = (bf16[8,3712]{1,0:T(8,128)(2,1)S(1)}, bf16[8,3712]{1,0:T(8,128)(2,1)S(1)}, u32[]{:S(2)}, u32[]{:S(2)}) collective-permute-start(bf16[8,3712]{1,0:T(8,128)(2,1)S(1)} %get-tuple-element.41), channel_id=1, source_target_pairs={{0,14},{2,12},{4,10},{6,8},{8,6},{10,4},{12,2},{14,0},{1,15},{3,13... | collective-permute-start | bytes 178184 | tf_op jit(solution)/shard_map/ppermute | solution.py:467
  23.1 17.5 %collective-permute-start.7 = (bf16[8,7680]{1,0:T(8,128)(2,1)S(1)}, bf16[8,7680]{1,0:T(8,128)(2,1)S(1)}, u32[]{:S(2)}, u32[]{:S(2)}) collective-permute-start(bf16[8,7680]{1,0:T(8,128)(2,1)S(1)} %get-tuple-element.45), channel_id=1, source_target_pairs={{0,4},{2,6},{4,0},{6,2},{8,12},{10,14},{12,8},{14,10},{1,5},{3,7},... | collective-permute-start | bytes 368648 | tf_op jit(solution)/shard_map/ppermute | solution.py:467
  24.8 11.1 %collective-permute-start.2 = (bf16[8,4224]{1,0:T(8,128)(2,1)S(1)}, bf16[8,4224]{1,0:T(8,128)(2,1)S(1)}, u32[]{:S(2)}, u32[]{:S(2)}) collective-permute-start(bf16[8,4224]{1,0:T(8,128)(2,1)S(1)} %get-tuple-element.37), channel_id=1, source_target_pairs={{0,6},{2,4},{4,2},{6,0},{8,14},{10,12},{12,10},{14,8},{1,7},{3,5},... | collective-permute-start | bytes 202760 | tf_op jit(solution)/shard_map/ppermute | solution.py:467
  32.0 8.6 %collective-permute-start.8 = (bf16[8,4096]{1,0:T(8,128)(2,1)S(1)}, bf16[8,4096]{1,0:T(8,128)(2,1)S(1)}, u32[]{:S(2)}, u32[]{:S(2)}) collective-permute-start(bf16[8,4096]{1,0:T(8,128)(2,1)S(1)} %get-tuple-element.46), channel_id=1, source_target_pairs={{0,8},{2,10},{4,12},{6,14},{8,0},{10,2},{12,4},{14,6},{1,9},{3,11}... | collective-permute-start | bytes 196616 | tf_op jit(solution)/shard_map/ppermute | solution.py:467
  41.7 1.3 %collective-permute-start.10 = (f32[64,128]{1,0:T(8,128)S(1)}, f32[64,128]{1,0:T(8,128)S(1)}, u32[]{:S(2)}, u32[]{:S(2)}) collective-permute-start(f32[64,128]{1,0:T(8,128)S(1)} %get-tuple-element.55.mine_ref), channel_id=1, source_target_pairs={{0,1},{1,0},{2,3},{3,2},{4,5},{5,4},{6,7},{7,6},{8,9},{9,8},{10,11... | collective-permute-start | bytes 98312 | tf_op jit(solution)/shard_map/ppermute | solution.py:571
